TPU v7x, 768 devices: a whole 4x8x12 slice. The times are simulated.
768 devices in a mesh: rep: 12 (over z), sp: 64 (over x, y, core).
Axes of the slice: x: 4, y: 8, z: 12, core: 2. Of those that a mesh axis runs over, the one named last changes fastest.
Arguments:
- inputs: bfloat16 [12, 64, 16, 4096], P('rep', 'sp'), may hold values from -6 to 6
- preact: bfloat16 [12, 64, 16, 4096], P('rep', 'sp'), may hold values from -6 to 6
- grad_out: bfloat16 [12, 64, 16, 4096], P('rep', 'sp'), may hold values from -20 to 20
- weight: bfloat16 [3, 3, 3, 64, 64], replicated, may hold values from -0.15625 to 0.15625
Outputs:
- input_grad: bfloat16 [12, 64, 16, 4096], P('rep', 'sp')
- weight_grad: float32 [3, 3, 3, 64, 64], replicated
- bias_grad: float32 [64], replicated
All inputs are finite; a program needn't handle non-finite values.
Results may differ from a plain program's by a relative error of at most 0.001.
Values may be sent and summed in bfloat16 or wider, within the bound.
No kernel may reach another device: no remote copies, remote signals or barrier semaphores. Data moves between devices by JAX's collectives and lax.ppermute only.
A program may use at most 32 MiB of HBM per device.

v0:
```python
import jax
import jax.numpy as jnp
from jax import lax
from jax.experimental import pallas as pl
from jax.experimental.pallas import tpu as pltpu
from jax.sharding import PartitionSpec as P


CH = 64
LANES = 2 * CH
CHUNK = 14
SMALL = pltpu.CompilerParams(vmem_limit_bytes=16 * 1024 * 1024)


def mask_kernel(preact_ref, grad_ref, x_ref, own_ref, pack_ref, z_ref, dy_ref, sems):
    height = own_ref.shape[0]
    loads = (
        pltpu.make_async_copy(preact_ref, z_ref, sems.at[0]),
        pltpu.make_async_copy(grad_ref, dy_ref, sems.at[1]),
        pltpu.make_async_copy(x_ref, pack_ref.at[height:], sems.at[2]),
    )
    for load in loads:
        load.start()
    loads[0].wait()
    loads[1].wait()
    own = jnp.where(z_ref[...] > 0, dy_ref[...], jnp.zeros_like(dy_ref))
    own_ref[...] = own
    pack_ref[0:height, :] = own
    loads[2].wait()


def inputs_kernel(pair_ref, xt_ref):
    height, packed = pair_ref.shape[0] // 2, pair_ref.shape[1]
    x_ref = pair_ref.at[height:]
    pairs = packed // LANES
    rows = pairs * height
    x = jnp.concatenate([x_ref[:, LANES * j : LANES * (j + 1)] for j in range(pairs)], axis=0)
    xt = jnp.transpose(x.astype(jnp.float32))
    h = lax.broadcasted_iota(jnp.int32, (LANES, rows), 1) % height
    xt_ref[0:LANES, :] = jnp.where(h == 0, 0.0, pltpu.roll(xt, 1, 1)).astype(jnp.bfloat16)
    xt_ref[LANES : 2 * LANES, :] = xt.astype(jnp.bfloat16)
    xt_ref[2 * LANES :, :] = jnp.where(h == height - 1, 0.0, pltpu.roll(xt, rows - 1, 1)).astype(jnp.bfloat16)


def weights_kernel(core_ref, w_ref, wt_ref):
    core = core_ref[0]
    zero = jnp.zeros((CH, CH), jnp.bfloat16)
    for slot, od in enumerate((2 - 2 * core, 1, 2 * core)):
        for oh in range(3):
            t = 9 * od + 3 * oh
            before, here, after = w_ref[t], w_ref[t + 1], w_ref[t + 2]
            for parity in range(2):
                if parity == 0:
                    parts = (here, before, zero, after)
                else:
                    parts = (after, here, before, zero)
                r = (2 * oh + parity) * CH
                wt_ref[r : r + CH, 256 * slot : 256 * slot + LANES] = jnp.concatenate(parts[:2], axis=1)
                wt_ref[r : r + CH, 256 * slot + LANES : 256 * (slot + 1)] = jnp.concatenate(parts[2:], axis=1)


def kernel_gradient_kernel(core_ref, far_ref, own_ref, near_ref, xt_own_ref, xt_near_ref, dw_ref, g_ref):
    height, packed = own_ref.shape
    pairs = packed // LANES
    low = lax.broadcasted_iota(jnp.int32, (height, LANES), 1) < CH
    for slot, ref in enumerate((far_ref, own_ref, near_ref)):
        for j in range(pairs):
            at = slice(height * j, height * (j + 1))
            g_ref[at, 256 * slot : 256 * slot + LANES] = ref[0:height, LANES * j : LANES * (j + 1)]
            nothing = jnp.zeros((height, LANES), jnp.bfloat16)
            right = ref[0:height, LANES * (j + 1) : LANES * (j + 2)] if j + 1 < pairs else nothing
            left = ref[0:height, LANES * (j - 1) : LANES * j] if j > 0 else nothing
            g_ref[at, 256 * slot + LANES : 256 * (slot + 1)] = jnp.where(low, right, left)
    d = jnp.dot(xt_own_ref[...], g_ref[:, 0:512], preferred_element_type=jnp.float32)
    d = d + jnp.dot(xt_near_ref[...], g_ref[:, 256:768], preferred_element_type=jnp.float32)
    lo = lax.broadcasted_iota(jnp.int32, (CH, LANES), 1) < CH
    core_0 = jnp.full((CH, LANES), core_ref[0], jnp.int32) == 0

    def block(part, oh, parity, half):
        r = LANES * oh + CH * parity
        c = 256 * part + LANES * half
        return d[r : r + CH, c : c + LANES]

    def swap(v):
        return pltpu.roll(v, CH, 1)

    def two(part, oh):
        return block(part, oh, 0, 0) + jnp.where(lo, swap(block(part, oh, 1, 0)), swap(block(part, oh, 1, 1)))

    def low_one(part, oh):
        return block(part, oh, 1, 0) + swap(block(part, oh, 0, 1))

    def high_one(part, oh):
        return swap(block(part, oh, 1, 0)) + block(part, oh, 0, 1)

    total = jnp.sum(g_ref[:, 256:384].astype(jnp.float32) + g_ref[:, 512:640].astype(jnp.float32), axis=0, keepdims=True)
    first = lax.broadcasted_iota(jnp.int32, (CH, LANES), 0) == 0
    bias = jnp.where(first, jnp.broadcast_to(total + swap(total), (CH, LANES)), 0.0)
    blocks = (
        two(0, 0),
        two(0, 1),
        two(0, 2),
        jnp.where(lo, low_one(0, 0), high_one(0, 1)),
        jnp.where(lo, low_one(0, 2), jnp.where(core_0, high_one(1, 0), high_one(1, 2))),
        jnp.where(core_0, two(1, 0), two(1, 2)),
        jnp.where(core_0, two(1, 1), jnp.where(lo, low_one(1, 1), bias)),
    )
    for i, v in enumerate(blocks):
        dw_ref[CH * i : CH * (i + 1), :] = v


def input_gradient_kernel(g_ref, wt_ref, dx_ref):
    height, packed = dx_ref.shape
    pairs = packed // LANES
    rows = pairs * height
    y = lax.dot_general(
        g_ref[...], wt_ref[...], (((1,), (1,)), ((), ())), preferred_element_type=jnp.float32
    )
    h = lax.broadcasted_iota(jnp.int32, (rows, LANES), 0) % height
    up = jnp.where(h == height - 1, 0.0, pltpu.roll(y[:, :LANES], rows - 1, 0))
    down = jnp.where(h == 0, 0.0, pltpu.roll(y[:, 2 * LANES :], 1, 0))
    out = (y[:, LANES : 2 * LANES] + up + down).astype(jnp.bfloat16)
    for j in range(pairs):
        dx_ref[:, LANES * j : LANES * (j + 1)] = out[height * j : height * (j + 1), :]


def sum_kernel(parts_ref, out_ref, *, scale):
    group = 4 * CHUNK
    total = parts_ref[0:group, :]
    for i in range(1, parts_ref.shape[0] // group):
        total = total + parts_ref[group * i : group * (i + 1), :]
    s = (total[0:CHUNK] + total[CHUNK : 2 * CHUNK]) + (total[2 * CHUNK : 3 * CHUNK] + total[3 * CHUNK :])
    s = s * scale
    four = jnp.concatenate([s, s, s, s], axis=0)
    for i in range(out_ref.shape[0] // group):
        out_ref[group * i : group * (i + 1), :] = four


def unpack_kernel(core_ref, mine_ref, other_ref, weight_ref, bias_ref):
    core_0 = jnp.full((CH, LANES), core_ref[0], jnp.int32) == 0
    places = (
        ((19, 18), (22, 21), (25, 24), (20, 23), (26, 11), (10, 9), (13, 12)),
        ((1, 0), (4, 3), (7, 6), (2, 5), (8, 17), (16, 15), (14, None)),
    )
    for half, sides in enumerate(places):
        for i, (lower, upper) in enumerate(sides):
            a = mine_ref[CH * i : CH * (i + 1), :]
            b = other_ref[CH * i : CH * (i + 1), :]
            v = jnp.where(core_0, a, b) if half == 0 else jnp.where(core_0, b, a)
            weight_ref[lower] = v[:, :CH]
            if upper is None:
                bias_ref[...] = v[0:1, CH:]
            else:
                weight_ref[upper] = v[:, CH:]


def in_vmem(array):
    return pltpu.with_memory_space_constraint(array, pltpu.VMEM)


def in_hbm(array):
    return pltpu.with_memory_space_constraint(array, pltpu.HBM)


def sum_and_copy(parts, copies, scale):
    return pl.pallas_call(
        lambda p, o: sum_kernel(p, o, scale=scale),
        out_shape=pltpu.VMEM((copies * CHUNK, LANES), jnp.float32),
        compiler_params=SMALL,
    )(in_vmem(parts))


def exchange(rows, axis):
    return lax.all_to_all(rows.reshape(-1, 1, LANES), axis, 0, 0, tiled=True).reshape(-1, LANES)


def on_device(inputs, preact, grad_out, weight):
    chips = lax.axis_size("chip")
    slabs = chips * lax.axis_size("core")
    groups = lax.axis_size("rep")
    _, planes, height, packed = inputs.shape
    count = inputs.shape[0] * groups * planes * slabs * height * (packed // CH)
    scale = 1.0 / float(count) ** 0.5
    core = lax.axis_index("core").astype(jnp.int32).reshape(1)
    in_smem = pl.BlockSpec(memory_space=pltpu.SMEM)
    whole = pl.BlockSpec(memory_space=pltpu.VMEM)
    rows = height * packed // LANES
    own, pack = pl.pallas_call(
        mask_kernel,
        in_specs=[pl.BlockSpec(memory_space=pltpu.HBM)] * 3,
        out_shape=(
            pltpu.VMEM((height, packed), jnp.bfloat16),
            pltpu.VMEM((2 * height, packed), jnp.bfloat16),
        ),
        scratch_shapes=[pltpu.VMEM((height, packed), jnp.bfloat16)] * 2 + [pltpu.SemaphoreType.DMA((3,))],
        compiler_params=SMALL,
        name="mask",
    )(*(in_hbm(a.reshape(height, packed)) for a in (preact, grad_out, inputs)))
    swap = [(0, 1), (1, 0)]
    ends = range(1, slabs - 1, 2)
    far = lax.ppermute(own, ("chip", "core"), [(i, i + 1) for i in ends] + [(i + 1, i) for i in ends])
    near = in_vmem(lax.ppermute(pack, "core", swap))
    wt = pl.pallas_call(
        weights_kernel,
        in_specs=[in_smem, whole],
        out_shape=pltpu.VMEM((3 * LANES, 768), jnp.bfloat16),
        compiler_params=SMALL,
        name="weights",
    )(core, weight.reshape(27, CH, CH))

    def turned(pair):
        return pl.pallas_call(
            inputs_kernel,
            out_shape=pltpu.VMEM((3 * LANES, rows), jnp.bfloat16),
            compiler_params=SMALL,
            name="inputs",
        )(in_vmem(pair))

    dw, g = pl.pallas_call(
        kernel_gradient_kernel,
        in_specs=[in_smem] + [whole] * 5,
        out_shape=(
            pltpu.VMEM((chips * CHUNK, LANES), jnp.float32),
            pltpu.VMEM((rows, 768), jnp.bfloat16),
        ),
        compiler_params=SMALL,
        name="kernel_gradient",
    )(core, in_vmem(far), in_vmem(own), near, in_vmem(turned(pack)), in_vmem(turned(near)))
    dx = pl.pallas_call(
        input_gradient_kernel,
        out_shape=jax.ShapeDtypeStruct((height, packed), jnp.bfloat16),
        compiler_params=SMALL,
        name="input_gradient",
    )(in_vmem(g), in_vmem(wt))
    mine = sum_and_copy(exchange(dw, "chip"), groups, 1.0)
    total = sum_and_copy(exchange(mine, "rep"), chips, scale)
    gathered = exchange(total, "chip")
    other = lax.ppermute(gathered, "core", swap)
    weight_grad, bias_grad = pl.pallas_call(
        unpack_kernel,
        in_specs=[in_smem, whole, whole],
        out_shape=(
            jax.ShapeDtypeStruct((27, CH, CH), jnp.float32),
            jax.ShapeDtypeStruct((1, CH), jnp.float32),
        ),
        compiler_params=SMALL,
        name="unpack",
    )(core, in_vmem(gathered), in_vmem(other))
    return dx.reshape(inputs.shape), weight_grad.reshape(3, 3, 3, CH, CH), bias_grad.reshape(CH)


def solution(mesh):
    groups, slabs = mesh.devices.shape
    by_core = jax.sharding.Mesh(mesh.devices.reshape(groups, slabs // 2, 2), ("rep", "chip", "core"))
    split = P("rep", ("chip", "core"), None, None)
    return jax.shard_map(
        on_device,
        mesh=by_core,
        in_specs=(split, split, split, P()),
        out_specs=(split, P(), P()),
        check_vma=False,
    )
```

profile of v0, /device:TPU:1, one launch (start us, length us, event | category | flops | bytes accessed | tf_op | source)
XLA Modules:
  0.0 80.6 jit_solution(11527066243535004488)
XLA Ops:
  0.6 1.1 %mask.1 = (bf16[16,4096]{1,0:T(8,128)(2,1)S(1)}, bf16[32,4096]{1,0:T(8,128)(2,1)S(1)}) custom-call(bf16[16,4096]{1,0:T(8,128)(2,1)} %bitcast.28, bf16[16,4096]{1,0:T(8,128)(2,1)} %bitcast.29, bf16[16,4096]{1,0:T(8,128)(2,1)} %bitcast.30), custom_call_target="tpu_custom_call" | custom-call | tf_op jit(solution)/shard_map/mask/pallas_call | solution.py:188
  1.7 12.4 %collective-permute-start.1 = (bf16[32,4096]{1,0:T(8,128)(2,1)S(1)}, bf16[32,4096]{1,0:T(8,128)(2,1)S(1)}, u32[]{:S(2)}, u32[]{:S(2)}) collective-permute-start(bf16[32,4096]{1,0:T(8,128)(2,1)S(1)} %get-tuple-element.10.pair_ref), channel_id=1, source_target_pairs={{0,1},{1,0},{2,3},{3,2},{4,5},{5,4},{6,7},{7,6},{8,9},{9,8},{10,11... | collective-permute-start | bytes 786440 | tf_op jit(solution)/shard_map/ppermute | solution.py:202
  14.1 1.9 %collective-permute-start = (bf16[16,4096]{1,0:T(8,128)(2,1)S(1)}, bf16[16,4096]{1,0:T(8,128)(2,1)S(1)}, u32[]{:S(2)}, u32[]{:S(2)}) collective-permute-start(bf16[16,4096]{1,0:T(8,128)(2,1)S(1)} %get-tuple-element.9.own_ref), channel_id=1, source_target_pairs={{1,2},{3,4},{5,6},{7,8},{9,10},{11,12},{13,14},{15,16},{17,18},{19... | collective-permute-start | bytes 393224 | tf_op jit(solution)/shard_map/ppermute | solution.py:201
  16.0 0.2 inputs.2.xt_own_ref
  16.3 0.0 collective-permute-done.1.pair_ref.near_ref
  16.3 0.2 inputs.3.xt_near_ref
  16.5 3.9 %collective-permute-done.far_ref = bf16[16,4096]{1,0:T(8,128)(2,1)S(1)} collective-permute-done((bf16[16,4096]{1,0:T(8,128)(2,1)S(1)}, bf16[16,4096]{1,0:T(8,128)(2,1)S(1)}, u32[]{:S(2)}, u32[]{:S(2)}) %collective-permute-start) | collective-permute-done | bytes 131104 | tf_op jit(solution)/shard_map/ppermute | solution.py:201
  20.4 0.7 kernel_gradient.1
  21.1 13.9 %all_to_all.15 = f32[448,1,128]{2,1,0:T(1,128)S(1)} all-to-all(f32[448,1,128]{2,1,0:T(1,128)S(1)} %bitcast.27), channel_id=1, replica_groups=mesh['rep'=12,'chip'=32,'core'=2] {'chip'}, dimensions={0} | all-to-all | bytes 458752 | tf_op jit(solution)/shard_map/all_to_all | solution.py:174
  35.1 0.0 copy-start
  35.1 21.2 %all_to_all.16 = f32[168,1,128]{2,1,0:T(1,128)S(1)} all-to-all(f32[168,1,128]{2,1,0:T(1,128)S(1)} %bitcast.25), channel_id=1, replica_groups=mesh['rep'=12,'chip'=32,'core'=2] {'rep'}, dimensions={0} | all-to-all | bytes 172032 | tf_op jit(solution)/shard_map/all_to_all | solution.py:174
  56.3 15.1 %all_to_all.17 = f32[448,1,128]{2,1,0:T(1,128)S(1)} all-to-all(f32[448,1,128]{2,1,0:T(1,128)S(1)} %bitcast.21), channel_id=1, replica_groups=mesh['rep'=12,'chip'=32,'core'=2] {'chip'}, dimensions={0} | all-to-all | bytes 458752 | tf_op jit(solution)/shard_map/all_to_all | solution.py:174
  71.4 6.6 %collective-permute-start.2 = (f32[448,128]{1,0:T(8,128)S(1)}, f32[448,128]{1,0:T(8,128)S(1)}, u32[]{:S(2)}, u32[]{:S(2)}) collective-permute-start(f32[448,128]{1,0:T(8,128)S(1)} %bitcast.22), channel_id=1, source_target_pairs={{0,1},{1,0},{2,3},{3,2},{4,5},{5,4},{6,7},{7,6},{8,9},{9,8},{10,11... | collective-permute-start | bytes 688136 | tf_op jit(solution)/shard_map/ppermute | solution.py:238
  78.0 0.0 copy-done
  78.0 0.2 weights.1.wt_ref
  78.2 1.3 %input_gradient.1 = bf16[16,4096]{1,0:T(8,128)(2,1)} custom-call(bf16[512,768]{1,0:T(8,128)(2,1)S(1)} %get-tuple-element.11.g_ref, bf16[384,768]{1,0:T(8,128)(2,1)S(1)} %weights.1.wt_ref), custom_call_target="tpu_custom_call" | custom-call | tf_op jit(solution)/shard_map/input_gradient/pallas_call | solution.py:229
  79.5 0.0 collective-permute-done.2.other_ref
  79.5 1.1 %unpack.1 = (f32[27,64,64]{2,1,0:T(8,128)}, f32[1,64]{1,0:T(1,128)}) custom-call(s32[1]{0:T(128)} %bitcast.core_ref, f32[448,128]{1,0:T(8,128)S(1)} %bitcast.23, f32[448,128]{1,0:T(8,128)S(1)} %collective-permute-done.2.other_ref), custom_call_target="tpu_custom_call" | custom-call | tf_op jit(solution)/shard_map/unpack/pallas_call | solution.py:239
  (2 shorter events, 0.1 us)
Async XLA Ops:
  1.7 14.6 %collective-permute-start.1 = (bf16[32,4096]{1,0:T(8,128)(2,1)S(1)}, bf16[32,4096]{1,0:T(8,128)(2,1)S(1)}, u32[]{:S(2)}, u32[]{:S(2)}) collective-permute-start(bf16[32,4096]{1,0:T(8,128)(2,1)S(1)} %get-tuple-element.10.pair_ref), channel_id=1, source_target_pairs={{0,1},{1,0},{2,3},{3,2},{4,5},{5,4},{6,7},{7,6},{8,9},{9,8},{10,11... | collective-permute-start | bytes 786440 | tf_op jit(solution)/shard_map/ppermute | solution.py:202
  14.1 6.3 %collective-permute-start = (bf16[16,4096]{1,0:T(8,128)(2,1)S(1)}, bf16[16,4096]{1,0:T(8,128)(2,1)S(1)}, u32[]{:S(2)}, u32[]{:S(2)}) collective-permute-start(bf16[16,4096]{1,0:T(8,128)(2,1)S(1)} %get-tuple-element.9.own_ref), channel_id=1, source_target_pairs={{1,2},{3,4},{5,6},{7,8},{9,10},{11,12},{13,14},{15,16},{17,18},{19... | collective-permute-start | bytes 393224 | tf_op jit(solution)/shard_map/ppermute | solution.py:201
  35.1 43.0 %copy-start = (bf16[3,3,3,64,64]{4,3,2,1,0:T(8,128)(2,1)S(1)}, bf16[3,3,3,64,64]{4,3,2,1,0:T(8,128)(2,1)}, u32[]{:S(2)}) copy-start(bf16[3,3,3,64,64]{4,3,2,1,0:T(8,128)(2,1)} %param.7) | copy-start | bytes 663556
  71.4 8.1 %collective-permute-start.2 = (f32[448,128]{1,0:T(8,128)S(1)}, f32[448,128]{1,0:T(8,128)S(1)}, u32[]{:S(2)}, u32[]{:S(2)}) collective-permute-start(f32[448,128]{1,0:T(8,128)S(1)} %bitcast.22), channel_id=1, source_target_pairs={{0,1},{1,0},{2,3},{3,2},{4,5},{5,4},{6,7},{7,6},{8,9},{9,8},{10,11... | collective-permute-start | bytes 688136 | tf_op jit(solution)/shard_map/ppermute | solution.py:238
where the time goes:
time: 80.9 us; the launch traced here: 80.6 us
  blocking collectives  50.2 us (62%)
  starting transfers between devices  20.9 us (26%)
  Pallas kernels  4.83 us (6%)
  waiting for transfers between devices  3.88 us (5%)
    all_to_all x3, blocking collectives, exchange(): lax.all_to_all(rows.reshape(-1, 1, LANES), axis, 0, 0, tiled=True)  50.2 us
    ppermute x1, starting transfers between devices, on_device(): near = in_vmem(lax.ppermute(pack, 'core', swap))  12.4 us
    ppermute x1, starting transfers between devices, on_device(): other = lax.ppermute(gathered, 'core', swap)  6.63 us
    ppermute x1, waiting for transfers between devices, on_device(): lax.ppermute(own, ('chip', 'core'), [(i, i + 1) for i in ends] + [(i + 1,...  3.88 us
    ppermute x1, starting transfers between devices, on_device(): lax.ppermute(own, ('chip', 'core'), [(i, i + 1) for i in ends] + [(i + 1,...  1.92 us
  transfers between devices with their start and end apart: 3, of which 1 were waited for; matrix products, arithmetic and copies ran while one was open for 0% of the time, Pallas kernels for 2%

commit v1 on v0

--- a/solution.py
+++ b/solution.py
@@ -8,6 +8,7 @@
 
 CH = 64
 LANES = 2 * CH
+SLOT = 16
 CHUNK = 14
 SMALL = pltpu.CompilerParams(vmem_limit_bytes=16 * 1024 * 1024)
 
@@ -124,19 +125,34 @@
         dx_ref[:, LANES * j : LANES * (j + 1)] = out[height * j : height * (j + 1), :]
 
 
-def sum_kernel(parts_ref, out_ref, *, scale):
+def sum_kernel(parts_ref, out_ref):
     group = 4 * CHUNK
     total = parts_ref[0:group, :]
     for i in range(1, parts_ref.shape[0] // group):
         total = total + parts_ref[group * i : group * (i + 1), :]
     s = (total[0:CHUNK] + total[CHUNK : 2 * CHUNK]) + (total[2 * CHUNK : 3 * CHUNK] + total[3 * CHUNK :])
-    s = s * scale
     four = jnp.concatenate([s, s, s, s], axis=0)
     for i in range(out_ref.shape[0] // group):
         out_ref[group * i : group * (i + 1), :] = four
 
 
-def unpack_kernel(core_ref, mine_ref, other_ref, weight_ref, bias_ref):
+def finish_kernel(parts_ref, out_ref, *, scale):
+    s = parts_ref[0:CHUNK, :]
+    for i in range(1, parts_ref.shape[0] // CHUNK):
+        s = s + parts_ref[CHUNK * i : CHUNK * (i + 1), :]
+    s = s * scale
+    largest = jnp.max(jnp.abs(s), axis=0, keepdims=True)
+    exponent = jnp.floor(jnp.log2(jnp.maximum(largest, 1e-30))) - 14.0
+    slot = jnp.concatenate([s * jnp.exp2(-exponent), exponent, jnp.zeros_like(exponent)], axis=0)
+    for i in range(out_ref.shape[0] // SLOT):
+        out_ref[SLOT * i : SLOT * (i + 1), :] = slot
+
+
+def unpack_kernel(core_ref, mine_slots_ref, other_slots_ref, weight_ref, bias_ref, mine_ref, other_ref):
+    for slots_ref, rows_ref in ((mine_slots_ref, mine_ref), (other_slots_ref, other_ref)):
+        for i in range(slots_ref.shape[0] // SLOT):
+            unit = jnp.exp2(slots_ref[SLOT * i + CHUNK : SLOT * i + CHUNK + 1, :])
+            rows_ref[CHUNK * i : CHUNK * (i + 1), :] = slots_ref[SLOT * i : SLOT * i + CHUNK, :] * unit
     core_0 = jnp.full((CH, LANES), core_ref[0], jnp.int32) == 0
     places = (
         ((19, 18), (22, 21), (25, 24), (20, 23), (26, 11), (10, 9), (13, 12)),
@@ -162,11 +178,9 @@
     return pltpu.with_memory_space_constraint(array, pltpu.HBM)
 
 
-def sum_and_copy(parts, copies, scale):
+def sum_and_copy(parts, copies):
     return pl.pallas_call(
-        lambda p, o: sum_kernel(p, o, scale=scale),
-        out_shape=pltpu.VMEM((copies * CHUNK, LANES), jnp.float32),
-        compiler_params=SMALL,
+        sum_kernel, out_shape=pltpu.VMEM((copies * CHUNK, LANES), jnp.float32), compiler_params=SMALL
     )(in_vmem(parts))
 
 
@@ -232,9 +246,14 @@
         compiler_params=SMALL,
         name="input_gradient",
     )(in_vmem(g), in_vmem(wt))
-    mine = sum_and_copy(exchange(dw, "chip"), groups, 1.0)
-    total = sum_and_copy(exchange(mine, "rep"), chips, scale)
-    gathered = exchange(total, "chip")
+    mine = sum_and_copy(exchange(dw, "chip"), groups)
+    total = pl.pallas_call(
+        lambda p, o: finish_kernel(p, o, scale=scale),
+        out_shape=pltpu.VMEM((chips * SLOT, LANES), jnp.float32),
+        compiler_params=SMALL,
+        name="finish",
+    )(in_vmem(exchange(mine, "rep")))
+    gathered = lax.all_to_all(total.astype(jnp.float16), "chip", 0, 0, tiled=True)
     other = lax.ppermute(gathered, "core", swap)
     weight_grad, bias_grad = pl.pallas_call(
         unpack_kernel,
@@ -243,9 +262,10 @@
             jax.ShapeDtypeStruct((27, CH, CH), jnp.float32),
             jax.ShapeDtypeStruct((1, CH), jnp.float32),
         ),
+        scratch_shapes=[pltpu.VMEM((chips * CHUNK, LANES), jnp.float32)] * 2,
         compiler_params=SMALL,
         name="unpack",
-    )(core, in_vmem(gathered), in_vmem(other))
+    )(core, in_vmem(gathered.astype(jnp.float32)), in_vmem(other.astype(jnp.float32)))
     return dx.reshape(inputs.shape), weight_grad.reshape(3, 3, 3, CH, CH), bias_grad.reshape(CH)
 
 

time: 80.9 us -> 80.8 us (level)
  blocking collectives: 50.2 us -> 35 us
  waiting for transfers between devices: 3.88 us -> 12.5 us
  starting transfers between devices: 20.9 us -> 26.6 us
    all_to_all x3 -> x2, blocking collectives: 50.2 us -> 35 us  [exchange(): lax.all_to_all(rows.reshape(-1, 1, LANES), axis, 0, 0, tiled=True)]
    all_to_all x0 -> x1, waiting for transfers between devices: none -> 7.72 us  [on_device(): lax.all_to_all(total.astype(jnp.float16), 'chip', 0, 0, tiled=True)]
    all_to_all x0 -> x1, starting transfers between devices: none -> 5.71 us  [on_device(): lax.all_to_all(total.astype(jnp.float16), 'chip', 0, 0, tiled=True)]
    ppermute x1, waiting for transfers between devices: 0.01 us -> 0.93 us  [on_device(): other = lax.ppermute(gathered, 'core', swap)]
  transfers between devices with their start and end apart: 3 -> 4, of which waited for: 1 -> 3; matrix products, arithmetic and copies ran while one was open for 0% -> 0% of each run, Pallas kernels for 2% -> 2%
where the time goes in v1:
time: 80.8 us; the launch traced here: 80.5 us
  blocking collectives  35 us (43%)
  starting transfers between devices  26.6 us (33%)
  waiting for transfers between devices  12.5 us (15%)
  Pallas kernels  4.87 us (6%)
    all_to_all x2, blocking collectives, exchange(): lax.all_to_all(rows.reshape(-1, 1, LANES), axis, 0, 0, tiled=True)  35 us
    ppermute x1, starting transfers between devices, on_device(): near = in_vmem(lax.ppermute(pack, 'core', swap))  12.4 us
    all_to_all x1, waiting for transfers between devices, on_device(): lax.all_to_all(total.astype(jnp.float16), 'chip', 0, 0, tiled=True)  7.72 us
    ppermute x1, starting transfers between devices, on_device(): other = lax.ppermute(gathered, 'core', swap)  6.61 us
    all_to_all x1, starting transfers between devices, on_device(): lax.all_to_all(total.astype(jnp.float16), 'chip', 0, 0, tiled=True)  5.71 us
    ppermute x1, waiting for transfers between devices, on_device(): lax.ppermute(own, ('chip', 'core'), [(i, i + 1) for i in ends] + [(i + 1,...  3.88 us
    ppermute x1, starting transfers between devices, on_device(): lax.ppermute(own, ('chip', 'core'), [(i, i + 1) for i in ends] + [(i + 1,...  1.92 us
  transfers between devices with their start and end apart: 4, of which 3 were waited for; matrix products, arithmetic and copies ran while one was open for 0% of the time, Pallas kernels for 2%

profile of v1, /device:TPU:1, one launch (start us, length us, event | category | flops | bytes accessed | tf_op | source)
XLA Modules:
  0.0 80.5 jit_solution(5638705968827293557)
XLA Ops:
  0.6 1.1 %mask.1 = (bf16[16,4096]{1,0:T(8,128)(2,1)S(1)}, bf16[32,4096]{1,0:T(8,128)(2,1)S(1)}) custom-call(bf16[16,4096]{1,0:T(8,128)(2,1)} %bitcast.25, bf16[16,4096]{1,0:T(8,128)(2,1)} %bitcast.26, bf16[16,4096]{1,0:T(8,128)(2,1)} %bitcast.27), custom_call_target="tpu_custom_call" | custom-call | tf_op jit(solution)/shard_map/mask/pallas_call | solution.py:202
  1.7 12.4 %collective-permute-start.1 = (bf16[32,4096]{1,0:T(8,128)(2,1)S(1)}, bf16[32,4096]{1,0:T(8,128)(2,1)S(1)}, u32[]{:S(2)}, u32[]{:S(2)}) collective-permute-start(bf16[32,4096]{1,0:T(8,128)(2,1)S(1)} %get-tuple-element.10.pair_ref), channel_id=1, source_target_pairs={{0,1},{1,0},{2,3},{3,2},{4,5},{5,4},{6,7},{7,6},{8,9},{9,8},{10,11... | collective-permute-start | bytes 786440 | tf_op jit(solution)/shard_map/ppermute | solution.py:216
  14.1 1.9 %collective-permute-start = (bf16[16,4096]{1,0:T(8,128)(2,1)S(1)}, bf16[16,4096]{1,0:T(8,128)(2,1)S(1)}, u32[]{:S(2)}, u32[]{:S(2)}) collective-permute-start(bf16[16,4096]{1,0:T(8,128)(2,1)S(1)} %get-tuple-element.9.own_ref), channel_id=1, source_target_pairs={{1,2},{3,4},{5,6},{7,8},{9,10},{11,12},{13,14},{15,16},{17,18},{19... | collective-permute-start | bytes 393224 | tf_op jit(solution)/shard_map/ppermute | solution.py:215
  16.0 0.2 inputs.2.xt_own_ref
  16.3 0.0 collective-permute-done.1.pair_ref.near_ref
  16.3 0.2 inputs.3.xt_near_ref
  16.5 3.9 %collective-permute-done.far_ref = bf16[16,4096]{1,0:T(8,128)(2,1)S(1)} collective-permute-done((bf16[16,4096]{1,0:T(8,128)(2,1)S(1)}, bf16[16,4096]{1,0:T(8,128)(2,1)S(1)}, u32[]{:S(2)}, u32[]{:S(2)}) %collective-permute-start) | collective-permute-done | bytes 131104 | tf_op jit(solution)/shard_map/ppermute | solution.py:215
  20.4 0.7 kernel_gradient.1
  21.1 13.9 %all_to_all.22 = f32[448,1,128]{2,1,0:T(1,128)S(1)} all-to-all(f32[448,1,128]{2,1,0:T(1,128)S(1)} %bitcast.23), channel_id=1, replica_groups=mesh['rep'=12,'chip'=32,'core'=2] {'chip'}, dimensions={0} | all-to-all | bytes 458752 | tf_op jit(solution)/shard_map/all_to_all | solution.py:188
  35.1 21.0 %all_to_all.23 = f32[168,1,128]{2,1,0:T(1,128)S(1)} all-to-all(f32[168,1,128]{2,1,0:T(1,128)S(1)} %bitcast.21), channel_id=1, replica_groups=mesh['rep'=12,'chip'=32,'core'=2] {'rep'}, dimensions={0} | all-to-all | bytes 172032 | tf_op jit(solution)/shard_map/all_to_all | solution.py:188
  56.1 0.0 copy-start
  56.1 0.1 finish.1
  56.2 0.7 convert_element_type.9
  56.8 5.7 %all-to-all-start.2 = ((f16[32,16,128]{2,1,0:T(8,128)(2,1)}), f16[32,16,128]{2,1,0:T(8,128)(2,1)S(1)}, u32[]{:S(2)}, u32[]{:S(2)}) async-start(f16[32,16,128]{2,1,0:T(8,128)(2,1)} %bitcast.12), calls=%async_computation.2 | async-start | bytes 262144 | tf_op jit(solution)/shard_map/all_to_all | solution.py:256
  62.6 0.0 copy-done
  62.6 0.2 weights.1.wt_ref
  62.8 1.3 %input_gradient.1 = bf16[16,4096]{1,0:T(8,128)(2,1)} custom-call(bf16[512,768]{1,0:T(8,128)(2,1)S(1)} %get-tuple-element.11.g_ref, bf16[384,768]{1,0:T(8,128)(2,1)S(1)} %weights.1.wt_ref), custom_call_target="tpu_custom_call" | custom-call | tf_op jit(solution)/shard_map/input_gradient/pallas_call | solution.py:243
  64.0 7.7 %all-to-all-done.2 = f16[32,16,128]{2,1,0:T(8,128)(2,1)S(1)} async-done(((f16[32,16,128]{2,1,0:T(8,128)(2,1)}), f16[32,16,128]{2,1,0:T(8,128)(2,1)S(1)}, u32[]{:S(2)}, u32[]{:S(2)}) %all-to-all-start.2) | async-done | bytes 131104 | tf_op jit(solution)/shard_map/all_to_all | solution.py:256
  71.7 6.6 %collective-permute-start.2 = (f16[512,128]{1,0:T(8,128)(2,1)S(1)}, f16[512,128]{1,0:T(8,128)(2,1)S(1)}, u32[]{:S(2)}, u32[]{:S(2)}) collective-permute-start(f16[512,128]{1,0:T(8,128)(2,1)S(1)} %bitcast.24), channel_id=1, source_target_pairs={{0,1},{1,0},{2,3},{3,2},{4,5},{5,4},{6,7},{7,6},{8,9},{9,8},{10,11... | collective-permute-start | bytes 393224 | tf_op jit(solution)/shard_map/ppermute | solution.py:257
  78.4 0.9 %collective-permute-done.2 = f16[512,128]{1,0:T(8,128)(2,1)S(1)} collective-permute-done((f16[512,128]{1,0:T(8,128)(2,1)S(1)}, f16[512,128]{1,0:T(8,128)(2,1)S(1)}, u32[]{:S(2)}, u32[]{:S(2)}) %collective-permute-start.2) | collective-permute-done | bytes 131104 | tf_op jit(solution)/shard_map/ppermute | solution.py:257
  79.3 1.1 %unpack.1 = (f32[27,64,64]{2,1,0:T(8,128)}, f32[1,64]{1,0:T(1,128)}) custom-call(s32[1]{0:T(128)} %bitcast.core_ref, f32[512,128]{1,0:T(8,128)S(1)} %bitcast_convert_fusion.mine_slots_ref, f32[512,128]{1,0:T(8,128)S(1)} %convert_element_type.11.other_slots_ref), custom_call_target="tpu_custom_call" | custom-call | tf_op jit(solution)/shard_map/unpack/pallas_call | solution.py:258
  (3 shorter events, 0.1 us)
Async XLA Ops:
  1.7 14.6 %collective-permute-start.1 = (bf16[32,4096]{1,0:T(8,128)(2,1)S(1)}, bf16[32,4096]{1,0:T(8,128)(2,1)S(1)}, u32[]{:S(2)}, u32[]{:S(2)}) collective-permute-start(bf16[32,4096]{1,0:T(8,128)(2,1)S(1)} %get-tuple-element.10.pair_ref), channel_id=1, source_target_pairs={{0,1},{1,0},{2,3},{3,2},{4,5},{5,4},{6,7},{7,6},{8,9},{9,8},{10,11... | collective-permute-start | bytes 786440 | tf_op jit(solution)/shard_map/ppermute | solution.py:216
  14.1 6.3 %collective-permute-start = (bf16[16,4096]{1,0:T(8,128)(2,1)S(1)}, bf16[16,4096]{1,0:T(8,128)(2,1)S(1)}, u32[]{:S(2)}, u32[]{:S(2)}) collective-permute-start(bf16[16,4096]{1,0:T(8,128)(2,1)S(1)} %get-tuple-element.9.own_ref), channel_id=1, source_target_pairs={{1,2},{3,4},{5,6},{7,8},{9,10},{11,12},{13,14},{15,16},{17,18},{19... | collective-permute-start | bytes 393224 | tf_op jit(solution)/shard_map/ppermute | solution.py:215
  56.1 6.5 %copy-start = (bf16[3,3,3,64,64]{4,3,2,1,0:T(8,128)(2,1)S(1)}, bf16[3,3,3,64,64]{4,3,2,1,0:T(8,128)(2,1)}, u32[]{:S(2)}) copy-start(bf16[3,3,3,64,64]{4,3,2,1,0:T(8,128)(2,1)} %param.7) | copy-start | bytes 663556
  56.8 14.9 %all-to-all-start.2 = ((f16[32,16,128]{2,1,0:T(8,128)(2,1)}), f16[32,16,128]{2,1,0:T(8,128)(2,1)S(1)}, u32[]{:S(2)}, u32[]{:S(2)}) async-start(f16[32,16,128]{2,1,0:T(8,128)(2,1)} %bitcast.12), calls=%async_computation.2 | async-start | bytes 262144 | tf_op jit(solution)/shard_map/all_to_all | solution.py:256
  71.7 7.6 %collective-permute-start.2 = (f16[512,128]{1,0:T(8,128)(2,1)S(1)}, f16[512,128]{1,0:T(8,128)(2,1)S(1)}, u32[]{:S(2)}, u32[]{:S(2)}) collective-permute-start(f16[512,128]{1,0:T(8,128)(2,1)S(1)} %bitcast.24), channel_id=1, source_target_pairs={{0,1},{1,0},{2,3},{3,2},{4,5},{5,4},{6,7},{7,6},{8,9},{9,8},{10,11... | collective-permute-start | bytes 393224 | tf_op jit(solution)/shard_map/ppermute | solution.py:257

commit v2 on v0

--- a/solution.py
+++ b/solution.py
@@ -8,6 +8,7 @@
 
 CH = 64
 LANES = 2 * CH
+SLOT = 16
 CHUNK = 14
 SMALL = pltpu.CompilerParams(vmem_limit_bytes=16 * 1024 * 1024)
 
@@ -124,29 +125,50 @@
         dx_ref[:, LANES * j : LANES * (j + 1)] = out[height * j : height * (j + 1), :]
 
 
-def sum_kernel(parts_ref, out_ref, *, scale):
+def to_slot(rows):
+    largest = jnp.max(jnp.abs(rows), axis=0, keepdims=True)
+    exponent = jnp.floor(jnp.log2(jnp.maximum(largest, 1e-30))) - 14.0
+    rest = [exponent, jnp.zeros((SLOT - CHUNK - 1, LANES), jnp.float32)]
+    return jnp.concatenate([rows * jnp.exp2(-exponent)] + rest, axis=0)
+
+
+def from_slot(slots_ref, i):
+    unit = jnp.exp2(slots_ref[SLOT * i + CHUNK : SLOT * i + CHUNK + 1, :])
+    return slots_ref[SLOT * i : SLOT * i + CHUNK, :] * unit
+
+
+def plane_sum_kernel(parts_ref, out_ref):
     group = 4 * CHUNK
     total = parts_ref[0:group, :]
     for i in range(1, parts_ref.shape[0] // group):
         total = total + parts_ref[group * i : group * (i + 1), :]
     s = (total[0:CHUNK] + total[CHUNK : 2 * CHUNK]) + (total[2 * CHUNK : 3 * CHUNK] + total[3 * CHUNK :])
-    s = s * scale
-    four = jnp.concatenate([s, s, s, s], axis=0)
-    for i in range(out_ref.shape[0] // group):
-        out_ref[group * i : group * (i + 1), :] = four
-
-
-def unpack_kernel(core_ref, mine_ref, other_ref, weight_ref, bias_ref):
-    core_0 = jnp.full((CH, LANES), core_ref[0], jnp.int32) == 0
+    slot = to_slot(s)
+    for i in range(out_ref.shape[0] // SLOT):
+        out_ref[SLOT * i : SLOT * (i + 1), :] = slot
+
+
+def finish_kernel(slots_ref, out_ref, *, scale):
+    for core in range(2):
+        s = from_slot(slots_ref, core)
+        for i in range(core + 2, slots_ref.shape[0] // SLOT, 2):
+            s = s + from_slot(slots_ref, i)
+        slot = to_slot(s * scale)
+        for i in range(core, out_ref.shape[0] // SLOT, 2):
+            out_ref[SLOT * i : SLOT * (i + 1), :] = slot
+
+
+def unpack_kernel(slots_ref, weight_ref, bias_ref, rows_ref):
+    chips = slots_ref.shape[0] // (2 * SLOT)
     places = (
         ((19, 18), (22, 21), (25, 24), (20, 23), (26, 11), (10, 9), (13, 12)),
         ((1, 0), (4, 3), (7, 6), (2, 5), (8, 17), (16, 15), (14, None)),
     )
-    for half, sides in enumerate(places):
+    for core, sides in enumerate(places):
+        for i in range(chips):
+            rows_ref[CHUNK * i : CHUNK * (i + 1), :] = from_slot(slots_ref, 2 * i + core)
         for i, (lower, upper) in enumerate(sides):
-            a = mine_ref[CH * i : CH * (i + 1), :]
-            b = other_ref[CH * i : CH * (i + 1), :]
-            v = jnp.where(core_0, a, b) if half == 0 else jnp.where(core_0, b, a)
+            v = rows_ref[CH * i : CH * (i + 1), :]
             weight_ref[lower] = v[:, :CH]
             if upper is None:
                 bias_ref[...] = v[0:1, CH:]
@@ -162,16 +184,9 @@
     return pltpu.with_memory_space_constraint(array, pltpu.HBM)
 
 
-def sum_and_copy(parts, copies, scale):
-    return pl.pallas_call(
-        lambda p, o: sum_kernel(p, o, scale=scale),
-        out_shape=pltpu.VMEM((copies * CHUNK, LANES), jnp.float32),
-        compiler_params=SMALL,
-    )(in_vmem(parts))
-
-
-def exchange(rows, axis):
-    return lax.all_to_all(rows.reshape(-1, 1, LANES), axis, 0, 0, tiled=True).reshape(-1, LANES)
+def exchange(slots, axis):
+    half = slots.astype(jnp.float16)
+    return in_vmem(lax.all_to_all(half, axis, 0, 0, tiled=True).astype(jnp.float32))
 
 
 def on_device(inputs, preact, grad_out, weight):
@@ -232,20 +247,29 @@
         compiler_params=SMALL,
         name="input_gradient",
     )(in_vmem(g), in_vmem(wt))
-    mine = sum_and_copy(exchange(dw, "chip"), groups, 1.0)
-    total = sum_and_copy(exchange(mine, "rep"), chips, scale)
-    gathered = exchange(total, "chip")
-    other = lax.ppermute(gathered, "core", swap)
+    parts = lax.all_to_all(dw.reshape(-1, 1, LANES), "chip", 0, 0, tiled=True).reshape(-1, LANES)
+    mine = pl.pallas_call(
+        plane_sum_kernel,
+        out_shape=pltpu.VMEM((groups * 2 * SLOT, LANES), jnp.float32),
+        compiler_params=SMALL,
+        name="plane_sum",
+    )(in_vmem(parts))
+    total = pl.pallas_call(
+        lambda p, o: finish_kernel(p, o, scale=scale),
+        out_shape=pltpu.VMEM((chips * 2 * SLOT, LANES), jnp.float32),
+        compiler_params=SMALL,
+        name="finish",
+    )(exchange(mine, ("rep", "core")))
     weight_grad, bias_grad = pl.pallas_call(
         unpack_kernel,
-        in_specs=[in_smem, whole, whole],
         out_shape=(
             jax.ShapeDtypeStruct((27, CH, CH), jnp.float32),
             jax.ShapeDtypeStruct((1, CH), jnp.float32),
         ),
+        scratch_shapes=[pltpu.VMEM((chips * CHUNK, LANES), jnp.float32)],
         compiler_params=SMALL,
         name="unpack",
-    )(core, in_vmem(gathered), in_vmem(other))
+    )(exchange(total, "chip"))
     return dx.reshape(inputs.shape), weight_grad.reshape(3, 3, 3, CH, CH), bias_grad.reshape(CH)
 
 

time: 80.9 us -> 79.3 us (0.980)
  the two profiles are of different devices: /device:TPU:1 before, /device:TPU:8 now
where the time goes in v2:
time: 79.3 us; the launch traced here: 79 us
  blocking collectives  41.4 us (52%)
  starting transfers between devices  18 us (23%)
  waiting for transfers between devices  13 us (16%)
  Pallas kernels  4.94 us (6%)
  other arithmetic  0.83 us (1%)
    all_to_all x1, blocking collectives, exchange(): lax.all_to_all(half, axis, 0, 0, tiled=True).astype(jnp.float32)  25.5 us
    all_to_all x1, blocking collectives, on_device(): lax.all_to_all(dw.reshape(-1, 1, LANES), 'chip', 0, 0, tiled=True)  15.9 us
    ppermute x1, starting transfers between devices, on_device(): lax.ppermute(own, ('chip', 'core'), [(i, i + 1) for i in ends] + [(i + 1,...  11.4 us
    all_to_all x1, waiting for transfers between devices, exchange(): lax.all_to_all(half, axis, 0, 0, tiled=True).astype(jnp.float32)  10.9 us
    all_to_all x1, starting transfers between devices, exchange(): lax.all_to_all(half, axis, 0, 0, tiled=True).astype(jnp.float32)  4.64 us
    ppermute x1, waiting for transfers between devices, on_device(): lax.ppermute(own, ('chip', 'core'), [(i, i + 1) for i in ends] + [(i + 1,...  2.16 us
    ppermute x1, starting transfers between devices, on_device(): near = in_vmem(lax.ppermute(pack, 'core', swap))  1.92 us
  transfers between devices with their start and end apart: 3, of which 2 were waited for; matrix products, arithmetic and copies ran while one was open for 0% of the time, Pallas kernels for 2%

profile of v2, /device:TPU:8, one launch (start us, length us, event | category | flops | bytes accessed | tf_op | source)
XLA Modules:
  0.0 79.0 jit_solution(9912157558324516757)
XLA Ops:
  0.6 1.1 %mask.1 = (bf16[16,4096]{1,0:T(8,128)(2,1)S(1)}, bf16[32,4096]{1,0:T(8,128)(2,1)S(1)}) custom-call(bf16[16,4096]{1,0:T(8,128)(2,1)} %bitcast.24, bf16[16,4096]{1,0:T(8,128)(2,1)} %bitcast.25, bf16[16,4096]{1,0:T(8,128)(2,1)} %bitcast.26), custom_call_target="tpu_custom_call" | custom-call | tf_op jit(solution)/shard_map/mask/pallas_call | solution.py:203
  1.7 1.9 %collective-permute-start.1 = (bf16[32,4096]{1,0:T(8,128)(2,1)S(1)}, bf16[32,4096]{1,0:T(8,128)(2,1)S(1)}, u32[]{:S(2)}, u32[]{:S(2)}) collective-permute-start(bf16[32,4096]{1,0:T(8,128)(2,1)S(1)} %get-tuple-element.10.pair_ref), channel_id=1, source_target_pairs={{0,1},{1,0},{2,3},{3,2},{4,5},{5,4},{6,7},{7,6},{8,9},{9,8},{10,11... | collective-permute-start | bytes 786440 | tf_op jit(solution)/shard_map/ppermute | solution.py:217
  3.6 11.4 %collective-permute-start = (bf16[16,4096]{1,0:T(8,128)(2,1)S(1)}, bf16[16,4096]{1,0:T(8,128)(2,1)S(1)}, u32[]{:S(2)}, u32[]{:S(2)}) collective-permute-start(bf16[16,4096]{1,0:T(8,128)(2,1)S(1)} %get-tuple-element.9.own_ref), channel_id=1, source_target_pairs={{1,2},{3,4},{5,6},{7,8},{9,10},{11,12},{13,14},{15,16},{17,18},{19... | collective-permute-start | bytes 393224 | tf_op jit(solution)/shard_map/ppermute | solution.py:216
  15.1 0.2 inputs.2.xt_own_ref
  15.3 0.0 collective-permute-done.1.pair_ref.near_ref
  15.3 0.2 inputs.3.xt_near_ref
  15.6 2.2 %collective-permute-done.far_ref = bf16[16,4096]{1,0:T(8,128)(2,1)S(1)} collective-permute-done((bf16[16,4096]{1,0:T(8,128)(2,1)S(1)}, bf16[16,4096]{1,0:T(8,128)(2,1)S(1)}, u32[]{:S(2)}, u32[]{:S(2)}) %collective-permute-start) | collective-permute-done | bytes 131104 | tf_op jit(solution)/shard_map/ppermute | solution.py:216
  17.7 0.7 kernel_gradient.1
  18.4 15.9 %all_to_all.23 = f32[448,1,128]{2,1,0:T(1,128)S(1)} all-to-all(f32[448,1,128]{2,1,0:T(1,128)S(1)} %bitcast.22), channel_id=1, replica_groups=mesh['rep'=12,'chip'=32,'core'=2] {'chip'}, dimensions={0} | all-to-all | bytes 458752 | tf_op jit(solution)/shard_map/all_to_all | solution.py:250
  34.3 0.1 plane_sum.1
  34.4 25.5 %all_to_all.24 = f16[24,16,128]{2,1,0:T(8,128)(2,1)S(1)} all-to-all(f16[24,16,128]{2,1,0:T(8,128)(2,1)S(1)} %bitcast.23), channel_id=1, replica_groups=mesh['rep'=12,'chip'=32,'core'=2] {'rep','core'}, dimensions={0} | all-to-all | bytes 196608 | tf_op jit(solution)/shard_map/all_to_all | solution.py:189
  60.0 0.1 finish.1
  60.1 0.7 convert_element_type.19
  60.8 0.0 copy-start
  60.8 4.6 %all-to-all-start.2 = ((f16[32,32,128]{2,1,0:T(8,128)(2,1)}), f16[32,32,128]{2,1,0:T(8,128)(2,1)S(1)}, u32[]{:S(2)}, u32[]{:S(2)}) async-start(f16[32,32,128]{2,1,0:T(8,128)(2,1)} %bitcast.11), calls=%async_computation.2 | async-start | bytes 524288 | tf_op jit(solution)/shard_map/all_to_all | solution.py:189
  65.5 0.0 copy-done
  65.5 0.2 weights.1.wt_ref
  65.7 1.3 %input_gradient.1 = bf16[16,4096]{1,0:T(8,128)(2,1)} custom-call(bf16[512,768]{1,0:T(8,128)(2,1)S(1)} %get-tuple-element.11.g_ref, bf16[384,768]{1,0:T(8,128)(2,1)S(1)} %weights.1.wt_ref), custom_call_target="tpu_custom_call" | custom-call | tf_op jit(solution)/shard_map/input_gradient/pallas_call | solution.py:244
  66.9 10.9 %all-to-all-done.2 = f16[32,32,128]{2,1,0:T(8,128)(2,1)S(1)} async-done(((f16[32,32,128]{2,1,0:T(8,128)(2,1)}), f16[32,32,128]{2,1,0:T(8,128)(2,1)S(1)}, u32[]{:S(2)}, u32[]{:S(2)}) %all-to-all-start.2) | async-done | bytes 262176 | tf_op jit(solution)/shard_map/all_to_all | solution.py:189
  77.8 0.1 bitcast_convert_fusion.slots_ref
  77.8 1.1 %unpack.1 = (f32[27,64,64]{2,1,0:T(8,128)}, f32[1,64]{1,0:T(1,128)}) custom-call(f32[1024,128]{1,0:T(8,128)S(1)} %bitcast_convert_fusion.slots_ref), custom_call_target="tpu_custom_call" | custom-call | tf_op jit(solution)/shard_map/unpack/pallas_call | solution.py:263
  (2 shorter events, 0.0 us)
Async XLA Ops:
  1.7 13.6 %collective-permute-start.1 = (bf16[32,4096]{1,0:T(8,128)(2,1)S(1)}, bf16[32,4096]{1,0:T(8,128)(2,1)S(1)}, u32[]{:S(2)}, u32[]{:S(2)}) collective-permute-start(bf16[32,4096]{1,0:T(8,128)(2,1)S(1)} %get-tuple-element.10.pair_ref), channel_id=1, source_target_pairs={{0,1},{1,0},{2,3},{3,2},{4,5},{5,4},{6,7},{7,6},{8,9},{9,8},{10,11... | collective-permute-start | bytes 786440 | tf_op jit(solution)/shard_map/ppermute | solution.py:217
  3.6 14.1 %collective-permute-start = (bf16[16,4096]{1,0:T(8,128)(2,1)S(1)}, bf16[16,4096]{1,0:T(8,128)(2,1)S(1)}, u32[]{:S(2)}, u32[]{:S(2)}) collective-permute-start(bf16[16,4096]{1,0:T(8,128)(2,1)S(1)} %get-tuple-element.9.own_ref), channel_id=1, source_target_pairs={{1,2},{3,4},{5,6},{7,8},{9,10},{11,12},{13,14},{15,16},{17,18},{19... | collective-permute-start | bytes 393224 | tf_op jit(solution)/shard_map/ppermute | solution.py:216
  60.8 4.6 %copy-start = (bf16[3,3,3,64,64]{4,3,2,1,0:T(8,128)(2,1)S(1)}, bf16[3,3,3,64,64]{4,3,2,1,0:T(8,128)(2,1)}, u32[]{:S(2)}) copy-start(bf16[3,3,3,64,64]{4,3,2,1,0:T(8,128)(2,1)} %param.7) | copy-start | bytes 663556
  60.8 17.0 %all-to-all-start.2 = ((f16[32,32,128]{2,1,0:T(8,128)(2,1)}), f16[32,32,128]{2,1,0:T(8,128)(2,1)S(1)}, u32[]{:S(2)}, u32[]{:S(2)}) async-start(f16[32,32,128]{2,1,0:T(8,128)(2,1)} %bitcast.11), calls=%async_computation.2 | async-start | bytes 524288 | tf_op jit(solution)/shard_map/all_to_all | solution.py:189

commit v3 on v1

--- a/solution.py
+++ b/solution.py
@@ -60,7 +60,7 @@
                 wt_ref[r : r + CH, 256 * slot + LANES : 256 * (slot + 1)] = jnp.concatenate(parts[2:], axis=1)
 
 
-def kernel_gradient_kernel(core_ref, far_ref, own_ref, near_ref, xt_own_ref, xt_near_ref, dw_ref, g_ref):
+def kernel_gradient_kernel(core_ref, far_ref, own_ref, near_ref, xt_own_ref, xt_near_ref, slots_ref, g_ref, dw_ref):
     height, packed = own_ref.shape
     pairs = packed // LANES
     low = lax.broadcasted_iota(jnp.int32, (height, LANES), 1) < CH
@@ -106,8 +106,15 @@
         jnp.where(core_0, two(1, 0), two(1, 2)),
         jnp.where(core_0, two(1, 1), jnp.where(lo, low_one(1, 1), bias)),
     )
+    largest = jnp.max(jnp.abs(blocks[0]), axis=0, keepdims=True)
+    for v in blocks[1:]:
+        largest = jnp.maximum(largest, jnp.max(jnp.abs(v), axis=0, keepdims=True))
+    exponent = exponents(largest)
+    unit = jnp.exp2(-exponent)
     for i, v in enumerate(blocks):
-        dw_ref[CH * i : CH * (i + 1), :] = v
+        dw_ref[CH * i : CH * (i + 1), :] = v * unit
+    for i in range(slots_ref.shape[0] // SLOT):
+        slots_ref[SLOT * i : SLOT * (i + 1), :] = to_slot(dw_ref[CHUNK * i : CHUNK * (i + 1), :], exponent)
 
 
 def input_gradient_kernel(g_ref, wt_ref, dx_ref):
@@ -125,15 +132,25 @@
         dx_ref[:, LANES * j : LANES * (j + 1)] = out[height * j : height * (j + 1), :]
 
 
-def sum_kernel(parts_ref, out_ref):
-    group = 4 * CHUNK
-    total = parts_ref[0:group, :]
-    for i in range(1, parts_ref.shape[0] // group):
-        total = total + parts_ref[group * i : group * (i + 1), :]
-    s = (total[0:CHUNK] + total[CHUNK : 2 * CHUNK]) + (total[2 * CHUNK : 3 * CHUNK] + total[3 * CHUNK :])
-    four = jnp.concatenate([s, s, s, s], axis=0)
-    for i in range(out_ref.shape[0] // group):
-        out_ref[group * i : group * (i + 1), :] = four
+def exponents(largest):
+    return jnp.floor(jnp.log2(jnp.maximum(largest, 1e-30))) - 14.0
+
+
+def to_slot(rows, exponent):
+    return jnp.concatenate([rows, exponent, jnp.zeros((SLOT - CHUNK - 1, LANES), jnp.float32)], axis=0)
+
+
+def from_slot(slots_ref, i):
+    unit = jnp.exp2(slots_ref[SLOT * i + CHUNK : SLOT * i + CHUNK + 1, :])
+    return slots_ref[SLOT * i : SLOT * i + CHUNK, :] * unit
+
+
+def plane_sum_kernel(slots_ref, out_ref):
+    sums = [from_slot(slots_ref, i) for i in range(slots_ref.shape[0] // SLOT)]
+    while len(sums) > 1:
+        sums = [a + b for a, b in zip(sums[::2], sums[1::2], strict=True)]
+    for i in range(out_ref.shape[0] // CHUNK):
+        out_ref[CHUNK * i : CHUNK * (i + 1), :] = sums[0]
 
 
 def finish_kernel(parts_ref, out_ref, *, scale):
@@ -141,9 +158,8 @@
     for i in range(1, parts_ref.shape[0] // CHUNK):
         s = s + parts_ref[CHUNK * i : CHUNK * (i + 1), :]
     s = s * scale
-    largest = jnp.max(jnp.abs(s), axis=0, keepdims=True)
-    exponent = jnp.floor(jnp.log2(jnp.maximum(largest, 1e-30))) - 14.0
-    slot = jnp.concatenate([s * jnp.exp2(-exponent), exponent, jnp.zeros_like(exponent)], axis=0)
+    exponent = exponents(jnp.max(jnp.abs(s), axis=0, keepdims=True))
+    slot = to_slot(s * jnp.exp2(-exponent), exponent)
     for i in range(out_ref.shape[0] // SLOT):
         out_ref[SLOT * i : SLOT * (i + 1), :] = slot
 
@@ -151,8 +167,7 @@
 def unpack_kernel(core_ref, mine_slots_ref, other_slots_ref, weight_ref, bias_ref, mine_ref, other_ref):
     for slots_ref, rows_ref in ((mine_slots_ref, mine_ref), (other_slots_ref, other_ref)):
         for i in range(slots_ref.shape[0] // SLOT):
-            unit = jnp.exp2(slots_ref[SLOT * i + CHUNK : SLOT * i + CHUNK + 1, :])
-            rows_ref[CHUNK * i : CHUNK * (i + 1), :] = slots_ref[SLOT * i : SLOT * i + CHUNK, :] * unit
+            rows_ref[CHUNK * i : CHUNK * (i + 1), :] = from_slot(slots_ref, i)
     core_0 = jnp.full((CH, LANES), core_ref[0], jnp.int32) == 0
     places = (
         ((19, 18), (22, 21), (25, 24), (20, 23), (26, 11), (10, 9), (13, 12)),
@@ -178,14 +193,12 @@
     return pltpu.with_memory_space_constraint(array, pltpu.HBM)
 
 
-def sum_and_copy(parts, copies):
-    return pl.pallas_call(
-        sum_kernel, out_shape=pltpu.VMEM((copies * CHUNK, LANES), jnp.float32), compiler_params=SMALL
-    )(in_vmem(parts))
-
-
 def exchange(rows, axis):
-    return lax.all_to_all(rows.reshape(-1, 1, LANES), axis, 0, 0, tiled=True).reshape(-1, LANES)
+    return in_vmem(lax.all_to_all(rows.reshape(-1, 1, LANES), axis, 0, 0, tiled=True).reshape(-1, LANES))
+
+
+def exchange_slots(slots):
+    return lax.all_to_all(slots.astype(jnp.float16), "chip", 0, 0, tiled=True)
 
 
 def on_device(inputs, preact, grad_out, weight):
@@ -234,27 +247,33 @@
         kernel_gradient_kernel,
         in_specs=[in_smem] + [whole] * 5,
         out_shape=(
-            pltpu.VMEM((chips * CHUNK, LANES), jnp.float32),
+            pltpu.VMEM((chips * SLOT, LANES), jnp.float32),
             pltpu.VMEM((rows, 768), jnp.bfloat16),
         ),
+        scratch_shapes=[pltpu.VMEM((chips * CHUNK, LANES), jnp.float32)],
         compiler_params=SMALL,
         name="kernel_gradient",
     )(core, in_vmem(far), in_vmem(own), near, in_vmem(turned(pack)), in_vmem(turned(near)))
+    mine = pl.pallas_call(
+        plane_sum_kernel,
+        out_shape=pltpu.VMEM((groups * CHUNK, LANES), jnp.float32),
+        compiler_params=SMALL,
+        name="plane_sum",
+    )(in_vmem(exchange_slots(dw).astype(jnp.float32)))
+    total = pl.pallas_call(
+        lambda p, o: finish_kernel(p, o, scale=scale),
+        out_shape=pltpu.VMEM((chips * SLOT, LANES), jnp.float32),
+        compiler_params=SMALL,
+        name="finish",
+    )(exchange(mine, "rep"))
+    gathered = exchange_slots(total)
+    other = lax.ppermute(gathered, "core", swap)
     dx = pl.pallas_call(
         input_gradient_kernel,
         out_shape=jax.ShapeDtypeStruct((height, packed), jnp.bfloat16),
         compiler_params=SMALL,
         name="input_gradient",
     )(in_vmem(g), in_vmem(wt))
-    mine = sum_and_copy(exchange(dw, "chip"), groups)
-    total = pl.pallas_call(
-        lambda p, o: finish_kernel(p, o, scale=scale),
-        out_shape=pltpu.VMEM((chips * SLOT, LANES), jnp.float32),
-        compiler_params=SMALL,
-        name="finish",
-    )(in_vmem(exchange(mine, "rep")))
-    gathered = lax.all_to_all(total.astype(jnp.float16), "chip", 0, 0, tiled=True)
-    other = lax.ppermute(gathered, "core", swap)
     weight_grad, bias_grad = pl.pallas_call(
         unpack_kernel,
         in_specs=[in_smem, whole, whole],

time: 80.8 us -> 79.2 us (0.980)
  starting transfers between devices: 26.6 us -> 25.3 us
    all_to_all x2 -> x1, blocking collectives: 35 us -> 21.4 us  [exchange(): lax.all_to_all(rows.reshape(-1, 1, LANES), axis, 0, 0, tiled=True)]
    all_to_all x0 -> x1, blocking collectives: none -> 13.1 us  [exchange_slots(): return lax.all_to_all(slots.astype(jnp.float16), 'chip', 0, 0, tiled=True)]
    all_to_all x1, starting transfers between devices: 5.71 us -> 3.86 us  [exchange_slots(): return lax.all_to_all(slots.astype(jnp.float16), 'chip', 0, 0, tiled=True)]
where the time goes in v3:
time: 79.2 us; the launch traced here: 78.9 us
  blocking collectives  34.5 us (44%)
  starting transfers between devices  25.3 us (32%)
  waiting for transfers between devices  12.5 us (16%)
  Pallas kernels  4.95 us (6%)
    all_to_all x1, blocking collectives, exchange(): lax.all_to_all(rows.reshape(-1, 1, LANES), axis, 0, 0, tiled=True)  21.4 us
    all_to_all x1, blocking collectives, exchange_slots(): return lax.all_to_all(slots.astype(jnp.float16), 'chip', 0, 0, tiled=True)  13.1 us
    ppermute x1, starting transfers between devices, on_device(): near = in_vmem(lax.ppermute(pack, 'core', swap))  12.4 us
    all_to_all x1, waiting for transfers between devices, exchange_slots(): return lax.all_to_all(slots.astype(jnp.float16), 'chip', 0, 0, tiled=True)  7.68 us
    ppermute x1, starting transfers between devices, on_device(): other = lax.ppermute(gathered, 'core', swap)  7.16 us
    ppermute x1, waiting for transfers between devices, on_device(): lax.ppermute(own, ('chip', 'core'), [(i, i + 1) for i in ends] + [(i + 1,...  3.88 us
    all_to_all x1, starting transfers between devices, exchange_slots(): return lax.all_to_all(slots.astype(jnp.float16), 'chip', 0, 0, tiled=True)  3.86 us
    ppermute x1, starting transfers between devices, on_device(): lax.ppermute(own, ('chip', 'core'), [(i, i + 1) for i in ends] + [(i + 1,...  1.92 us
  transfers between devices with their start and end apart: 4, of which 3 were waited for; matrix products, arithmetic and copies ran while one was open for 0% of the time, Pallas kernels for 2%

profile of v3, /device:TPU:1, one launch (start us, length us, event | category | flops | bytes accessed | tf_op | source)
XLA Modules:
  0.0 78.9 jit_solution(18408580469313104022)
XLA Ops:
  0.6 1.1 %mask.1 = (bf16[16,4096]{1,0:T(8,128)(2,1)S(1)}, bf16[32,4096]{1,0:T(8,128)(2,1)S(1)}) custom-call(bf16[16,4096]{1,0:T(8,128)(2,1)} %bitcast.24, bf16[16,4096]{1,0:T(8,128)(2,1)} %bitcast.25, bf16[16,4096]{1,0:T(8,128)(2,1)} %bitcast.26), custom_call_target="tpu_custom_call" | custom-call | tf_op jit(solution)/shard_map/mask/pallas_call | solution.py:215
  1.7 12.4 %collective-permute-start.1 = (bf16[32,4096]{1,0:T(8,128)(2,1)S(1)}, bf16[32,4096]{1,0:T(8,128)(2,1)S(1)}, u32[]{:S(2)}, u32[]{:S(2)}) collective-permute-start(bf16[32,4096]{1,0:T(8,128)(2,1)S(1)} %get-tuple-element.10.pair_ref), channel_id=1, source_target_pairs={{0,1},{1,0},{2,3},{3,2},{4,5},{5,4},{6,7},{7,6},{8,9},{9,8},{10,11... | collective-permute-start | bytes 786440 | tf_op jit(solution)/shard_map/ppermute | solution.py:229
  14.1 1.9 %collective-permute-start = (bf16[16,4096]{1,0:T(8,128)(2,1)S(1)}, bf16[16,4096]{1,0:T(8,128)(2,1)S(1)}, u32[]{:S(2)}, u32[]{:S(2)}) collective-permute-start(bf16[16,4096]{1,0:T(8,128)(2,1)S(1)} %get-tuple-element.9.own_ref), channel_id=1, source_target_pairs={{1,2},{3,4},{5,6},{7,8},{9,10},{11,12},{13,14},{15,16},{17,18},{19... | collective-permute-start | bytes 393224 | tf_op jit(solution)/shard_map/ppermute | solution.py:228
  16.0 0.2 inputs.2.xt_own_ref
  16.3 0.0 collective-permute-done.1.pair_ref.near_ref
  16.3 0.2 inputs.3.xt_near_ref
  16.5 3.9 %collective-permute-done.far_ref = bf16[16,4096]{1,0:T(8,128)(2,1)S(1)} collective-permute-done((bf16[16,4096]{1,0:T(8,128)(2,1)S(1)}, bf16[16,4096]{1,0:T(8,128)(2,1)S(1)}, u32[]{:S(2)}, u32[]{:S(2)}) %collective-permute-start) | collective-permute-done | bytes 131104 | tf_op jit(solution)/shard_map/ppermute | solution.py:228
  20.4 0.8 kernel_gradient.1
  21.2 13.1 %all_to_all.26 = f16[32,16,128]{2,1,0:T(8,128)(2,1)S(1)} all-to-all(f16[32,16,128]{2,1,0:T(8,128)(2,1)S(1)} %bitcast.23), channel_id=1, replica_groups=mesh['rep'=12,'chip'=32,'core'=2] {'chip'}, dimensions={0} | all-to-all | bytes 262144 | tf_op jit(solution)/shard_map/all_to_all | solution.py:201
  34.4 21.4 %all_to_all.27 = f32[168,1,128]{2,1,0:T(1,128)S(1)} all-to-all(f32[168,1,128]{2,1,0:T(1,128)S(1)} %bitcast.20), channel_id=1, replica_groups=mesh['rep'=12,'chip'=32,'core'=2] {'rep'}, dimensions={0} | all-to-all | bytes 172032 | tf_op jit(solution)/shard_map/all_to_all | solution.py:197
  55.8 0.0 copy-start
  55.8 0.1 finish.1
  55.9 0.7 convert_element_type.20
  56.5 3.9 %all-to-all-start.2 = ((f16[32,16,128]{2,1,0:T(8,128)(2,1)}), f16[32,16,128]{2,1,0:T(8,128)(2,1)S(1)}, u32[]{:S(2)}, u32[]{:S(2)}) async-start(f16[32,16,128]{2,1,0:T(8,128)(2,1)} %bitcast.11), calls=%async_computation.2 | async-start | bytes 262144 | tf_op jit(solution)/shard_map/all_to_all | solution.py:201
  60.4 0.0 copy-done
  60.4 0.2 weights.1.wt_ref
  60.6 1.3 %input_gradient.1 = bf16[16,4096]{1,0:T(8,128)(2,1)} custom-call(bf16[512,768]{1,0:T(8,128)(2,1)S(1)} %get-tuple-element.11.g_ref, bf16[384,768]{1,0:T(8,128)(2,1)S(1)} %weights.1.wt_ref), custom_call_target="tpu_custom_call" | custom-call | tf_op jit(solution)/shard_map/input_gradient/pallas_call | solution.py:271
  61.9 7.7 %all-to-all-done.2 = f16[32,16,128]{2,1,0:T(8,128)(2,1)S(1)} async-done(((f16[32,16,128]{2,1,0:T(8,128)(2,1)}), f16[32,16,128]{2,1,0:T(8,128)(2,1)S(1)}, u32[]{:S(2)}, u32[]{:S(2)}) %all-to-all-start.2) | async-done | bytes 131104 | tf_op jit(solution)/shard_map/all_to_all | solution.py:201
  69.6 7.2 %collective-permute-start.2 = (f16[512,128]{1,0:T(8,128)(2,1)S(1)}, f16[512,128]{1,0:T(8,128)(2,1)S(1)}, u32[]{:S(2)}, u32[]{:S(2)}) collective-permute-start(f16[512,128]{1,0:T(8,128)(2,1)S(1)} %bitcast.22), channel_id=1, source_target_pairs={{0,1},{1,0},{2,3},{3,2},{4,5},{5,4},{6,7},{7,6},{8,9},{9,8},{10,11... | collective-permute-start | bytes 393224 | tf_op jit(solution)/shard_map/ppermute | solution.py:270
  76.8 0.9 %collective-permute-done.2 = f16[512,128]{1,0:T(8,128)(2,1)S(1)} collective-permute-done((f16[512,128]{1,0:T(8,128)(2,1)S(1)}, f16[512,128]{1,0:T(8,128)(2,1)S(1)}, u32[]{:S(2)}, u32[]{:S(2)}) %collective-permute-start.2) | collective-permute-done | bytes 131104 | tf_op jit(solution)/shard_map/ppermute | solution.py:270
  77.7 1.1 %unpack.1 = (f32[27,64,64]{2,1,0:T(8,128)}, f32[1,64]{1,0:T(1,128)}) custom-call(s32[1]{0:T(128)} %bitcast.core_ref, f32[512,128]{1,0:T(8,128)S(1)} %bitcast_convert_fusion.1.mine_slots_ref, f32[512,128]{1,0:T(8,128)S(1)} %convert_element_type.22.other_slots_ref), custom_call_target="tpu_custom_call" | custom-call | tf_op jit(solution)/shard_map/unpack/pallas_call | solution.py:277
  (5 shorter events, 0.1 us)
Async XLA Ops:
  1.7 14.6 %collective-permute-start.1 = (bf16[32,4096]{1,0:T(8,128)(2,1)S(1)}, bf16[32,4096]{1,0:T(8,128)(2,1)S(1)}, u32[]{:S(2)}, u32[]{:S(2)}) collective-permute-start(bf16[32,4096]{1,0:T(8,128)(2,1)S(1)} %get-tuple-element.10.pair_ref), channel_id=1, source_target_pairs={{0,1},{1,0},{2,3},{3,2},{4,5},{5,4},{6,7},{7,6},{8,9},{9,8},{10,11... | collective-permute-start | bytes 786440 | tf_op jit(solution)/shard_map/ppermute | solution.py:229
  14.1 6.3 %collective-permute-start = (bf16[16,4096]{1,0:T(8,128)(2,1)S(1)}, bf16[16,4096]{1,0:T(8,128)(2,1)S(1)}, u32[]{:S(2)}, u32[]{:S(2)}) collective-permute-start(bf16[16,4096]{1,0:T(8,128)(2,1)S(1)} %get-tuple-element.9.own_ref), channel_id=1, source_target_pairs={{1,2},{3,4},{5,6},{7,8},{9,10},{11,12},{13,14},{15,16},{17,18},{19... | collective-permute-start | bytes 393224 | tf_op jit(solution)/shard_map/ppermute | solution.py:228
  55.8 4.6 %copy-start = (bf16[3,3,3,64,64]{4,3,2,1,0:T(8,128)(2,1)S(1)}, bf16[3,3,3,64,64]{4,3,2,1,0:T(8,128)(2,1)}, u32[]{:S(2)}) copy-start(bf16[3,3,3,64,64]{4,3,2,1,0:T(8,128)(2,1)} %param.7) | copy-start | bytes 663556
  56.5 13.0 %all-to-all-start.2 = ((f16[32,16,128]{2,1,0:T(8,128)(2,1)}), f16[32,16,128]{2,1,0:T(8,128)(2,1)S(1)}, u32[]{:S(2)}, u32[]{:S(2)}) async-start(f16[32,16,128]{2,1,0:T(8,128)(2,1)} %bitcast.11), calls=%async_computation.2 | async-start | bytes 262144 | tf_op jit(solution)/shard_map/all_to_all | solution.py:201
  69.6 8.1 %collective-permute-start.2 = (f16[512,128]{1,0:T(8,128)(2,1)S(1)}, f16[512,128]{1,0:T(8,128)(2,1)S(1)}, u32[]{:S(2)}, u32[]{:S(2)}) collective-permute-start(f16[512,128]{1,0:T(8,128)(2,1)S(1)} %bitcast.22), channel_id=1, source_target_pairs={{0,1},{1,0},{2,3},{3,2},{4,5},{5,4},{6,7},{7,6},{8,9},{9,8},{10,11... | collective-permute-start | bytes 393224 | tf_op jit(solution)/shard_map/ppermute | solution.py:270

commit v4 on v3

--- a/solution.py
+++ b/solution.py
@@ -164,25 +164,38 @@
         out_ref[SLOT * i : SLOT * (i + 1), :] = slot
 
 
-def unpack_kernel(core_ref, mine_slots_ref, other_slots_ref, weight_ref, bias_ref, mine_ref, other_ref):
-    for slots_ref, rows_ref in ((mine_slots_ref, mine_ref), (other_slots_ref, other_ref)):
-        for i in range(slots_ref.shape[0] // SLOT):
-            rows_ref[CHUNK * i : CHUNK * (i + 1), :] = from_slot(slots_ref, i)
-    core_0 = jnp.full((CH, LANES), core_ref[0], jnp.int32) == 0
+def unpack_kernel(
+    core_ref, mine_ref, other_ref, dx_ref, weight_ref, bias_ref, dx_out_ref, rows_ref, taps_ref, last_ref, sems
+):
+    stores = [pltpu.make_async_copy(dx_ref, dx_out_ref, sems.at[0])]
+    stores[0].start()
+    chips = mine_ref.shape[0] // SLOT
     places = (
-        ((19, 18), (22, 21), (25, 24), (20, 23), (26, 11), (10, 9), (13, 12)),
-        ((1, 0), (4, 3), (7, 6), (2, 5), (8, 17), (16, 15), (14, None)),
-    )
-    for half, sides in enumerate(places):
+        (((19, 18), (22, 21), (25, 24), (20, 23), (26, 11), (10, 9), (13, 12)), ((18, 27), (9, 14))),
+        (((1, 0), (4, 3), (7, 6), (2, 5), (8, 17), (16, 15), (14, None)), ((0, 9), (14, 18))),
+    )
+    core_0 = jnp.full((SLOT, LANES), core_ref[0], jnp.int32) == 0
+    for core, (sides, ranges) in enumerate(places):
+        for i in range(chips):
+            a = mine_ref[SLOT * i : SLOT * (i + 1), :]
+            b = other_ref[SLOT * i : SLOT * (i + 1), :]
+            v = jnp.where(core_0, a, b) if core == 0 else jnp.where(core_0, b, a)
+            rows_ref[CHUNK * i : CHUNK * (i + 1), :] = v[:CHUNK] * jnp.exp2(v[CHUNK : CHUNK + 1])
         for i, (lower, upper) in enumerate(sides):
-            a = mine_ref[CH * i : CH * (i + 1), :]
-            b = other_ref[CH * i : CH * (i + 1), :]
-            v = jnp.where(core_0, a, b) if half == 0 else jnp.where(core_0, b, a)
-            weight_ref[lower] = v[:, :CH]
+            v = rows_ref[CH * i : CH * (i + 1), :]
+            taps_ref[lower] = v[:, :CH]
             if upper is None:
-                bias_ref[...] = v[0:1, CH:]
+                last_ref[...] = v[0:1, CH:]
+                stores.append(pltpu.make_async_copy(last_ref, bias_ref, sems.at[len(stores)]))
+                stores[-1].start()
             else:
-                weight_ref[upper] = v[:, CH:]
+                taps_ref[upper] = v[:, CH:]
+        for first, end in ranges:
+            part = pl.ds(first, end - first)
+            stores.append(pltpu.make_async_copy(taps_ref.at[part], weight_ref.at[part], sems.at[len(stores)]))
+            stores[-1].start()
+    for store in stores:
+        store.wait()
 
 
 def in_vmem(array):
@@ -270,21 +283,28 @@
     other = lax.ppermute(gathered, "core", swap)
     dx = pl.pallas_call(
         input_gradient_kernel,
-        out_shape=jax.ShapeDtypeStruct((height, packed), jnp.bfloat16),
+        out_shape=pltpu.VMEM((height, packed), jnp.bfloat16),
         compiler_params=SMALL,
         name="input_gradient",
     )(in_vmem(g), in_vmem(wt))
-    weight_grad, bias_grad = pl.pallas_call(
+    weight_grad, bias_grad, dx = pl.pallas_call(
         unpack_kernel,
-        in_specs=[in_smem, whole, whole],
+        in_specs=[in_smem, whole, whole, whole],
+        out_specs=[pl.BlockSpec(memory_space=pltpu.HBM)] * 3,
         out_shape=(
             jax.ShapeDtypeStruct((27, CH, CH), jnp.float32),
             jax.ShapeDtypeStruct((1, CH), jnp.float32),
+            jax.ShapeDtypeStruct((height, packed), jnp.bfloat16),
         ),
-        scratch_shapes=[pltpu.VMEM((chips * CHUNK, LANES), jnp.float32)] * 2,
+        scratch_shapes=[
+            pltpu.VMEM((chips * CHUNK, LANES), jnp.float32),
+            pltpu.VMEM((27, CH, CH), jnp.float32),
+            pltpu.VMEM((1, CH), jnp.float32),
+            pltpu.SemaphoreType.DMA((6,)),
+        ],
         compiler_params=SMALL,
         name="unpack",
-    )(core, in_vmem(gathered.astype(jnp.float32)), in_vmem(other.astype(jnp.float32)))
+    )(core, in_vmem(gathered.astype(jnp.float32)), in_vmem(other.astype(jnp.float32)), in_vmem(dx))
     return dx.reshape(inputs.shape), weight_grad.reshape(3, 3, 3, CH, CH), bias_grad.reshape(CH)
 
 

time: 79.2 us -> 79.2 us (level)
  no operation moved by 1% of the time
where the time goes in v4:
time: 79.2 us; the launch traced here: 78.8 us
  blocking collectives  34.5 us (44%)
  starting transfers between devices  25.3 us (32%)
  waiting for transfers between devices  13.1 us (17%)
  Pallas kernels  4.27 us (5%)
    all_to_all x1, blocking collectives, exchange(): lax.all_to_all(rows.reshape(-1, 1, LANES), axis, 0, 0, tiled=True)  21.4 us
    all_to_all x1, blocking collectives, exchange_slots(): return lax.all_to_all(slots.astype(jnp.float16), 'chip', 0, 0, tiled=True)  13.1 us
    ppermute x1, starting transfers between devices, on_device(): near = in_vmem(lax.ppermute(pack, 'core', swap))  12.4 us
    all_to_all x1, waiting for transfers between devices, exchange_slots(): return lax.all_to_all(slots.astype(jnp.float16), 'chip', 0, 0, tiled=True)  8.34 us
    ppermute x1, starting transfers between devices, on_device(): other = lax.ppermute(gathered, 'core', swap)  7.17 us
    ppermute x1, waiting for transfers between devices, on_device(): lax.ppermute(own, ('chip', 'core'), [(i, i + 1) for i in ends] + [(i + 1,...  3.88 us
    all_to_all x1, starting transfers between devices, exchange_slots(): return lax.all_to_all(slots.astype(jnp.float16), 'chip', 0, 0, tiled=True)  3.86 us
    ppermute x1, starting transfers between devices, on_device(): lax.ppermute(own, ('chip', 'core'), [(i, i + 1) for i in ends] + [(i + 1,...  1.92 us
  transfers between devices with their start and end apart: 4, of which 3 were waited for; matrix products, arithmetic and copies ran while one was open for 0% of the time, Pallas kernels for 2%

profile of v4, /device:TPU:1, one launch (start us, length us, event | category | flops | bytes accessed | tf_op | source)
XLA Modules:
  0.0 78.8 jit_solution(15733645939913550900)
XLA Ops:
  0.6 1.1 %mask.1 = (bf16[16,4096]{1,0:T(8,128)(2,1)S(1)}, bf16[32,4096]{1,0:T(8,128)(2,1)S(1)}) custom-call(bf16[16,4096]{1,0:T(8,128)(2,1)} %bitcast.24, bf16[16,4096]{1,0:T(8,128)(2,1)} %bitcast.25, bf16[16,4096]{1,0:T(8,128)(2,1)} %bitcast.26), custom_call_target="tpu_custom_call" | custom-call | tf_op jit(solution)/shard_map/mask/pallas_call | solution.py:228
  1.7 12.4 %collective-permute-start.1 = (bf16[32,4096]{1,0:T(8,128)(2,1)S(1)}, bf16[32,4096]{1,0:T(8,128)(2,1)S(1)}, u32[]{:S(2)}, u32[]{:S(2)}) collective-permute-start(bf16[32,4096]{1,0:T(8,128)(2,1)S(1)} %get-tuple-element.11.pair_ref), channel_id=1, source_target_pairs={{0,1},{1,0},{2,3},{3,2},{4,5},{5,4},{6,7},{7,6},{8,9},{9,8},{10,11... | collective-permute-start | bytes 786440 | tf_op jit(solution)/shard_map/ppermute | solution.py:242
  14.1 1.9 %collective-permute-start = (bf16[16,4096]{1,0:T(8,128)(2,1)S(1)}, bf16[16,4096]{1,0:T(8,128)(2,1)S(1)}, u32[]{:S(2)}, u32[]{:S(2)}) collective-permute-start(bf16[16,4096]{1,0:T(8,128)(2,1)S(1)} %get-tuple-element.10.own_ref), channel_id=1, source_target_pairs={{1,2},{3,4},{5,6},{7,8},{9,10},{11,12},{13,14},{15,16},{17,18},{19... | collective-permute-start | bytes 393224 | tf_op jit(solution)/shard_map/ppermute | solution.py:241
  16.0 0.2 inputs.2.xt_own_ref
  16.3 0.0 collective-permute-done.1.pair_ref.near_ref
  16.3 0.2 inputs.3.xt_near_ref
  16.5 3.9 %collective-permute-done.far_ref = bf16[16,4096]{1,0:T(8,128)(2,1)S(1)} collective-permute-done((bf16[16,4096]{1,0:T(8,128)(2,1)S(1)}, bf16[16,4096]{1,0:T(8,128)(2,1)S(1)}, u32[]{:S(2)}, u32[]{:S(2)}) %collective-permute-start) | collective-permute-done | bytes 131104 | tf_op jit(solution)/shard_map/ppermute | solution.py:241
  20.4 0.8 kernel_gradient.1
  21.2 13.1 %all_to_all.26 = f16[32,16,128]{2,1,0:T(8,128)(2,1)S(1)} all-to-all(f16[32,16,128]{2,1,0:T(8,128)(2,1)S(1)} %bitcast.23), channel_id=1, replica_groups=mesh['rep'=12,'chip'=32,'core'=2] {'chip'}, dimensions={0} | all-to-all | bytes 262144 | tf_op jit(solution)/shard_map/all_to_all | solution.py:214
  34.4 21.4 %all_to_all.27 = f32[168,1,128]{2,1,0:T(1,128)S(1)} all-to-all(f32[168,1,128]{2,1,0:T(1,128)S(1)} %bitcast.20), channel_id=1, replica_groups=mesh['rep'=12,'chip'=32,'core'=2] {'rep'}, dimensions={0} | all-to-all | bytes 172032 | tf_op jit(solution)/shard_map/all_to_all | solution.py:210
  55.8 0.0 copy-start
  55.8 0.1 finish.1
  55.9 0.7 convert_element_type.20
  56.5 3.9 %all-to-all-start.2 = ((f16[32,16,128]{2,1,0:T(8,128)(2,1)}), f16[32,16,128]{2,1,0:T(8,128)(2,1)S(1)}, u32[]{:S(2)}, u32[]{:S(2)}) async-start(f16[32,16,128]{2,1,0:T(8,128)(2,1)} %bitcast.9), calls=%async_computation.2 | async-start | bytes 262144 | tf_op jit(solution)/shard_map/all_to_all | solution.py:214
  60.4 0.0 copy-done
  60.4 0.2 weights.1.wt_ref
  60.6 0.6 input_gradient.1.dx_ref
  61.2 8.3 %all-to-all-done.2 = f16[32,16,128]{2,1,0:T(8,128)(2,1)S(1)} async-done(((f16[32,16,128]{2,1,0:T(8,128)(2,1)}), f16[32,16,128]{2,1,0:T(8,128)(2,1)S(1)}, u32[]{:S(2)}, u32[]{:S(2)}) %all-to-all-start.2) | async-done | bytes 131104 | tf_op jit(solution)/shard_map/all_to_all | solution.py:214
  69.5 7.2 %collective-permute-start.2 = (f16[512,128]{1,0:T(8,128)(2,1)S(1)}, f16[512,128]{1,0:T(8,128)(2,1)S(1)}, u32[]{:S(2)}, u32[]{:S(2)}) collective-permute-start(f16[512,128]{1,0:T(8,128)(2,1)S(1)} %bitcast.22), channel_id=1, source_target_pairs={{0,1},{1,0},{2,3},{3,2},{4,5},{5,4},{6,7},{7,6},{8,9},{9,8},{10,11... | collective-permute-start | bytes 393224 | tf_op jit(solution)/shard_map/ppermute | solution.py:283
  76.8 0.9 %collective-permute-done.2 = f16[512,128]{1,0:T(8,128)(2,1)S(1)} collective-permute-done((f16[512,128]{1,0:T(8,128)(2,1)S(1)}, f16[512,128]{1,0:T(8,128)(2,1)S(1)}, u32[]{:S(2)}, u32[]{:S(2)}) %collective-permute-start.2) | collective-permute-done | bytes 131104 | tf_op jit(solution)/shard_map/ppermute | solution.py:283
  77.7 1.1 %unpack.1 = (f32[27,64,64]{2,1,0:T(8,128)}, f32[1,64]{1,0:T(1,128)}, bf16[16,4096]{1,0:T(8,128)(2,1)}) custom-call(s32[1]{0:T(128)} %bitcast.core_ref, f32[512,128]{1,0:T(8,128)S(1)} %bitcast_convert_fusion.1.mine_ref, f32[512,128]{1,0:T(8,128)S(1)} %convert_element_type.22.other_ref, bf16[16,4096]{1,0:T(8,128)(2,1)S(1)} %input_gradient.1.dx_ref), custom_call_target="tpu_custom_call" | custom-call | tf_op jit(solution)/shard_map/unpack/pallas_call | solution.py:290
  (5 shorter events, 0.1 us)
Async XLA Ops:
  1.7 14.6 %collective-permute-start.1 = (bf16[32,4096]{1,0:T(8,128)(2,1)S(1)}, bf16[32,4096]{1,0:T(8,128)(2,1)S(1)}, u32[]{:S(2)}, u32[]{:S(2)}) collective-permute-start(bf16[32,4096]{1,0:T(8,128)(2,1)S(1)} %get-tuple-element.11.pair_ref), channel_id=1, source_target_pairs={{0,1},{1,0},{2,3},{3,2},{4,5},{5,4},{6,7},{7,6},{8,9},{9,8},{10,11... | collective-permute-start | bytes 786440 | tf_op jit(solution)/shard_map/ppermute | solution.py:242
  14.1 6.3 %collective-permute-start = (bf16[16,4096]{1,0:T(8,128)(2,1)S(1)}, bf16[16,4096]{1,0:T(8,128)(2,1)S(1)}, u32[]{:S(2)}, u32[]{:S(2)}) collective-permute-start(bf16[16,4096]{1,0:T(8,128)(2,1)S(1)} %get-tuple-element.10.own_ref), channel_id=1, source_target_pairs={{1,2},{3,4},{5,6},{7,8},{9,10},{11,12},{13,14},{15,16},{17,18},{19... | collective-permute-start | bytes 393224 | tf_op jit(solution)/shard_map/ppermute | solution.py:241
  55.8 4.6 %copy-start = (bf16[3,3,3,64,64]{4,3,2,1,0:T(8,128)(2,1)S(1)}, bf16[3,3,3,64,64]{4,3,2,1,0:T(8,128)(2,1)}, u32[]{:S(2)}) copy-start(bf16[3,3,3,64,64]{4,3,2,1,0:T(8,128)(2,1)} %param.7) | copy-start | bytes 663556
  56.5 13.0 %all-to-all-start.2 = ((f16[32,16,128]{2,1,0:T(8,128)(2,1)}), f16[32,16,128]{2,1,0:T(8,128)(2,1)S(1)}, u32[]{:S(2)}, u32[]{:S(2)}) async-start(f16[32,16,128]{2,1,0:T(8,128)(2,1)} %bitcast.9), calls=%async_computation.2 | async-start | bytes 262144 | tf_op jit(solution)/shard_map/all_to_all | solution.py:214
  69.5 8.1 %collective-permute-start.2 = (f16[512,128]{1,0:T(8,128)(2,1)S(1)}, f16[512,128]{1,0:T(8,128)(2,1)S(1)}, u32[]{:S(2)}, u32[]{:S(2)}) collective-permute-start(f16[512,128]{1,0:T(8,128)(2,1)S(1)} %bitcast.22), channel_id=1, source_target_pairs={{0,1},{1,0},{2,3},{3,2},{4,5},{5,4},{6,7},{7,6},{8,9},{9,8},{10,11... | collective-permute-start | bytes 393224 | tf_op jit(solution)/shard_map/ppermute | solution.py:283

commit v5 on v4

--- a/solution.py
+++ b/solution.py
@@ -145,19 +145,12 @@
     return slots_ref[SLOT * i : SLOT * i + CHUNK, :] * unit
 
 
-def plane_sum_kernel(slots_ref, out_ref):
+def sum_kernel(slots_ref, out_ref, *, scale):
     sums = [from_slot(slots_ref, i) for i in range(slots_ref.shape[0] // SLOT)]
     while len(sums) > 1:
-        sums = [a + b for a, b in zip(sums[::2], sums[1::2], strict=True)]
-    for i in range(out_ref.shape[0] // CHUNK):
-        out_ref[CHUNK * i : CHUNK * (i + 1), :] = sums[0]
-
-
-def finish_kernel(parts_ref, out_ref, *, scale):
-    s = parts_ref[0:CHUNK, :]
-    for i in range(1, parts_ref.shape[0] // CHUNK):
-        s = s + parts_ref[CHUNK * i : CHUNK * (i + 1), :]
-    s = s * scale
+        pairs = [a + b for a, b in zip(sums[::2], sums[1::2])]
+        sums = pairs + sums[2 * len(pairs) :]
+    s = sums[0] * scale
     exponent = exponents(jnp.max(jnp.abs(s), axis=0, keepdims=True))
     slot = to_slot(s * jnp.exp2(-exponent), exponent)
     for i in range(out_ref.shape[0] // SLOT):
@@ -206,12 +199,17 @@
     return pltpu.with_memory_space_constraint(array, pltpu.HBM)
 
 
-def exchange(rows, axis):
-    return in_vmem(lax.all_to_all(rows.reshape(-1, 1, LANES), axis, 0, 0, tiled=True).reshape(-1, LANES))
-
-
-def exchange_slots(slots):
-    return lax.all_to_all(slots.astype(jnp.float16), "chip", 0, 0, tiled=True)
+def exchange(slots, axis):
+    return lax.all_to_all(slots.astype(jnp.float16), axis, 0, 0, tiled=True)
+
+
+def sum_slots(slots, copies, scale):
+    return pl.pallas_call(
+        lambda s, o: sum_kernel(s, o, scale=scale),
+        out_shape=pltpu.VMEM((copies * SLOT, LANES), jnp.float32),
+        compiler_params=SMALL,
+        name="sum_slots",
+    )(in_vmem(slots.astype(jnp.float32)))
 
 
 def on_device(inputs, preact, grad_out, weight):
@@ -267,19 +265,9 @@
         compiler_params=SMALL,
         name="kernel_gradient",
     )(core, in_vmem(far), in_vmem(own), near, in_vmem(turned(pack)), in_vmem(turned(near)))
-    mine = pl.pallas_call(
-        plane_sum_kernel,
-        out_shape=pltpu.VMEM((groups * CHUNK, LANES), jnp.float32),
-        compiler_params=SMALL,
-        name="plane_sum",
-    )(in_vmem(exchange_slots(dw).astype(jnp.float32)))
-    total = pl.pallas_call(
-        lambda p, o: finish_kernel(p, o, scale=scale),
-        out_shape=pltpu.VMEM((chips * SLOT, LANES), jnp.float32),
-        compiler_params=SMALL,
-        name="finish",
-    )(exchange(mine, "rep"))
-    gathered = exchange_slots(total)
+    mine = sum_slots(exchange(dw, "chip"), groups, 1.0)
+    total = sum_slots(exchange(mine, "rep"), chips, scale)
+    gathered = exchange(total, "chip")
     other = lax.ppermute(gathered, "core", swap)
     dx = pl.pallas_call(
         input_gradient_kernel,

time: 79.2 us -> 78.6 us (level)
  no operation moved by 1% of the time
where the time goes in v5:
time: 78.6 us; the launch traced here: 78.3 us
  blocking collectives  34.3 us (44%)
  starting transfers between devices  25 us (32%)
  waiting for transfers between devices  13.1 us (17%)
  Pallas kernels  4.29 us (5%)
  other arithmetic  0.8 us (1%)
  between operations  0.79 us (1%)
    all_to_all x2, blocking collectives, exchange(): return lax.all_to_all(slots.astype(jnp.float16), axis, 0, 0, tiled=True)  34.3 us
    ppermute x1, starting transfers between devices, on_device(): near = in_vmem(lax.ppermute(pack, 'core', swap))  12.4 us
    all_to_all x1, waiting for transfers between devices, exchange(): return lax.all_to_all(slots.astype(jnp.float16), axis, 0, 0, tiled=True)  8.34 us
    ppermute x1, starting transfers between devices, on_device(): other = lax.ppermute(gathered, 'core', swap)  6.81 us
    ppermute x1, waiting for transfers between devices, on_device(): lax.ppermute(own, ('chip', 'core'), [(i, i + 1) for i in ends] + [(i + 1,...  3.88 us
    all_to_all x1, starting transfers between devices, exchange(): return lax.all_to_all(slots.astype(jnp.float16), axis, 0, 0, tiled=True)  3.86 us
    ppermute x1, starting transfers between devices, on_device(): lax.ppermute(own, ('chip', 'core'), [(i, i + 1) for i in ends] + [(i + 1,...  1.92 us
  transfers between devices with their start and end apart: 4, of which 3 were waited for; matrix products, arithmetic and copies ran while one was open for 0% of the time, Pallas kernels for 2%

profile of v5, /device:TPU:1, one launch (start us, length us, event | category | flops | bytes accessed | tf_op | source)
XLA Modules:
  0.0 78.3 jit_solution(13138946066319416875)
XLA Ops:
  0.6 1.1 %mask.1 = (bf16[16,4096]{1,0:T(8,128)(2,1)S(1)}, bf16[32,4096]{1,0:T(8,128)(2,1)S(1)}) custom-call(bf16[16,4096]{1,0:T(8,128)(2,1)} %bitcast.23, bf16[16,4096]{1,0:T(8,128)(2,1)} %bitcast.24, bf16[16,4096]{1,0:T(8,128)(2,1)} %bitcast.25), custom_call_target="tpu_custom_call" | custom-call | tf_op jit(solution)/shard_map/mask/pallas_call | solution.py:226
  1.7 12.4 %collective-permute-start.1 = (bf16[32,4096]{1,0:T(8,128)(2,1)S(1)}, bf16[32,4096]{1,0:T(8,128)(2,1)S(1)}, u32[]{:S(2)}, u32[]{:S(2)}) collective-permute-start(bf16[32,4096]{1,0:T(8,128)(2,1)S(1)} %get-tuple-element.11.pair_ref), channel_id=1, source_target_pairs={{0,1},{1,0},{2,3},{3,2},{4,5},{5,4},{6,7},{7,6},{8,9},{9,8},{10,11... | collective-permute-start | bytes 786440 | tf_op jit(solution)/shard_map/ppermute | solution.py:240
  14.1 1.9 %collective-permute-start = (bf16[16,4096]{1,0:T(8,128)(2,1)S(1)}, bf16[16,4096]{1,0:T(8,128)(2,1)S(1)}, u32[]{:S(2)}, u32[]{:S(2)}) collective-permute-start(bf16[16,4096]{1,0:T(8,128)(2,1)S(1)} %get-tuple-element.10.own_ref), channel_id=1, source_target_pairs={{1,2},{3,4},{5,6},{7,8},{9,10},{11,12},{13,14},{15,16},{17,18},{19... | collective-permute-start | bytes 393224 | tf_op jit(solution)/shard_map/ppermute | solution.py:239
  16.0 0.2 inputs.2.xt_own_ref
  16.3 0.0 collective-permute-done.1.pair_ref.near_ref
  16.3 0.2 inputs.3.xt_near_ref
  16.5 3.9 %collective-permute-done.far_ref = bf16[16,4096]{1,0:T(8,128)(2,1)S(1)} collective-permute-done((bf16[16,4096]{1,0:T(8,128)(2,1)S(1)}, bf16[16,4096]{1,0:T(8,128)(2,1)S(1)}, u32[]{:S(2)}, u32[]{:S(2)}) %collective-permute-start) | collective-permute-done | bytes 131104 | tf_op jit(solution)/shard_map/ppermute | solution.py:239
  20.4 0.8 kernel_gradient.1
  21.2 13.1 %all_to_all.30 = f16[32,16,128]{2,1,0:T(8,128)(2,1)S(1)} all-to-all(f16[32,16,128]{2,1,0:T(8,128)(2,1)S(1)} %bitcast.21), channel_id=1, replica_groups=mesh['rep'=12,'chip'=32,'core'=2] {'chip'}, dimensions={0} | all-to-all | bytes 262144 | tf_op jit(solution)/shard_map/all_to_all | solution.py:203
  34.3 0.1 sum_slots.2
  34.4 21.2 %all_to_all.31 = f16[12,16,128]{2,1,0:T(8,128)(2,1)S(1)} all-to-all(f16[12,16,128]{2,1,0:T(8,128)(2,1)S(1)} %bitcast.22), channel_id=1, replica_groups=mesh['rep'=12,'chip'=32,'core'=2] {'rep'}, dimensions={0} | all-to-all | bytes 98304 | tf_op jit(solution)/shard_map/all_to_all | solution.py:203
  55.6 0.0 copy-start
  55.6 0.1 sum_slots.3
  55.7 0.7 convert_element_type.31
  56.4 3.9 %all-to-all-start.2 = ((f16[32,16,128]{2,1,0:T(8,128)(2,1)}), f16[32,16,128]{2,1,0:T(8,128)(2,1)S(1)}, u32[]{:S(2)}, u32[]{:S(2)}) async-start(f16[32,16,128]{2,1,0:T(8,128)(2,1)} %bitcast.8), calls=%async_computation.2 | async-start | bytes 262144 | tf_op jit(solution)/shard_map/all_to_all | solution.py:203
  60.2 0.0 copy-done
  60.3 0.2 weights.1.wt_ref
  60.4 0.6 input_gradient.1.dx_ref
  61.0 8.3 %all-to-all-done.2 = f16[32,16,128]{2,1,0:T(8,128)(2,1)S(1)} async-done(((f16[32,16,128]{2,1,0:T(8,128)(2,1)}), f16[32,16,128]{2,1,0:T(8,128)(2,1)S(1)}, u32[]{:S(2)}, u32[]{:S(2)}) %all-to-all-start.2) | async-done | bytes 131104 | tf_op jit(solution)/shard_map/all_to_all | solution.py:203
  69.4 6.8 %collective-permute-start.2 = (f16[512,128]{1,0:T(8,128)(2,1)S(1)}, f16[512,128]{1,0:T(8,128)(2,1)S(1)}, u32[]{:S(2)}, u32[]{:S(2)}) collective-permute-start(f16[512,128]{1,0:T(8,128)(2,1)S(1)} %bitcast.20), channel_id=1, source_target_pairs={{0,1},{1,0},{2,3},{3,2},{4,5},{5,4},{6,7},{7,6},{8,9},{9,8},{10,11... | collective-permute-start | bytes 393224 | tf_op jit(solution)/shard_map/ppermute | solution.py:271
  76.2 0.9 %collective-permute-done.2 = f16[512,128]{1,0:T(8,128)(2,1)S(1)} collective-permute-done((f16[512,128]{1,0:T(8,128)(2,1)S(1)}, f16[512,128]{1,0:T(8,128)(2,1)S(1)}, u32[]{:S(2)}, u32[]{:S(2)}) %collective-permute-start.2) | collective-permute-done | bytes 131104 | tf_op jit(solution)/shard_map/ppermute | solution.py:271
  77.2 1.1 %unpack.1 = (f32[27,64,64]{2,1,0:T(8,128)}, f32[1,64]{1,0:T(1,128)}, bf16[16,4096]{1,0:T(8,128)(2,1)}) custom-call(s32[1]{0:T(128)} %bitcast.core_ref, f32[512,128]{1,0:T(8,128)S(1)} %bitcast_convert_fusion.2.mine_ref, f32[512,128]{1,0:T(8,128)S(1)} %convert_element_type.33.other_ref, bf16[16,4096]{1,0:T(8,128)(2,1)S(1)} %input_gradient.1.dx_ref), custom_call_target="tpu_custom_call" | custom-call | tf_op jit(solution)/shard_map/unpack/pallas_call | solution.py:278
  (6 shorter events, 0.1 us)
Async XLA Ops:
  1.7 14.6 %collective-permute-start.1 = (bf16[32,4096]{1,0:T(8,128)(2,1)S(1)}, bf16[32,4096]{1,0:T(8,128)(2,1)S(1)}, u32[]{:S(2)}, u32[]{:S(2)}) collective-permute-start(bf16[32,4096]{1,0:T(8,128)(2,1)S(1)} %get-tuple-element.11.pair_ref), channel_id=1, source_target_pairs={{0,1},{1,0},{2,3},{3,2},{4,5},{5,4},{6,7},{7,6},{8,9},{9,8},{10,11... | collective-permute-start | bytes 786440 | tf_op jit(solution)/shard_map/ppermute | solution.py:240
  14.1 6.3 %collective-permute-start = (bf16[16,4096]{1,0:T(8,128)(2,1)S(1)}, bf16[16,4096]{1,0:T(8,128)(2,1)S(1)}, u32[]{:S(2)}, u32[]{:S(2)}) collective-permute-start(bf16[16,4096]{1,0:T(8,128)(2,1)S(1)} %get-tuple-element.10.own_ref), channel_id=1, source_target_pairs={{1,2},{3,4},{5,6},{7,8},{9,10},{11,12},{13,14},{15,16},{17,18},{19... | collective-permute-start | bytes 393224 | tf_op jit(solution)/shard_map/ppermute | solution.py:239
  55.6 4.6 %copy-start = (bf16[3,3,3,64,64]{4,3,2,1,0:T(8,128)(2,1)S(1)}, bf16[3,3,3,64,64]{4,3,2,1,0:T(8,128)(2,1)}, u32[]{:S(2)}) copy-start(bf16[3,3,3,64,64]{4,3,2,1,0:T(8,128)(2,1)} %param.7) | copy-start | bytes 663556
  56.4 13.0 %all-to-all-start.2 = ((f16[32,16,128]{2,1,0:T(8,128)(2,1)}), f16[32,16,128]{2,1,0:T(8,128)(2,1)S(1)}, u32[]{:S(2)}, u32[]{:S(2)}) async-start(f16[32,16,128]{2,1,0:T(8,128)(2,1)} %bitcast.8), calls=%async_computation.2 | async-start | bytes 262144 | tf_op jit(solution)/shard_map/all_to_all | solution.py:203
  69.4 7.8 %collective-permute-start.2 = (f16[512,128]{1,0:T(8,128)(2,1)S(1)}, f16[512,128]{1,0:T(8,128)(2,1)S(1)}, u32[]{:S(2)}, u32[]{:S(2)}) collective-permute-start(f16[512,128]{1,0:T(8,128)(2,1)S(1)} %bitcast.20), channel_id=1, source_target_pairs={{0,1},{1,0},{2,3},{3,2},{4,5},{5,4},{6,7},{7,6},{8,9},{9,8},{10,11... | collective-permute-start | bytes 393224 | tf_op jit(solution)/shard_map/ppermute | solution.py:271

commit v6 on v3

--- a/solution.py
+++ b/solution.py
@@ -60,27 +60,40 @@
                 wt_ref[r : r + CH, 256 * slot + LANES : 256 * (slot + 1)] = jnp.concatenate(parts[2:], axis=1)
 
 
-def kernel_gradient_kernel(core_ref, far_ref, own_ref, near_ref, xt_own_ref, xt_near_ref, slots_ref, g_ref, dw_ref):
-    height, packed = own_ref.shape
+def lay_out(ref, g_ref, column):
+    height, packed = g_ref.shape[0] * LANES // ref.shape[1], ref.shape[1]
     pairs = packed // LANES
     low = lax.broadcasted_iota(jnp.int32, (height, LANES), 1) < CH
-    for slot, ref in enumerate((far_ref, own_ref, near_ref)):
-        for j in range(pairs):
-            at = slice(height * j, height * (j + 1))
-            g_ref[at, 256 * slot : 256 * slot + LANES] = ref[0:height, LANES * j : LANES * (j + 1)]
-            nothing = jnp.zeros((height, LANES), jnp.bfloat16)
-            right = ref[0:height, LANES * (j + 1) : LANES * (j + 2)] if j + 1 < pairs else nothing
-            left = ref[0:height, LANES * (j - 1) : LANES * j] if j > 0 else nothing
-            g_ref[at, 256 * slot + LANES : 256 * (slot + 1)] = jnp.where(low, right, left)
-    d = jnp.dot(xt_own_ref[...], g_ref[:, 0:512], preferred_element_type=jnp.float32)
-    d = d + jnp.dot(xt_near_ref[...], g_ref[:, 256:768], preferred_element_type=jnp.float32)
+    nothing = jnp.zeros((height, LANES), jnp.bfloat16)
+    for j in range(pairs):
+        at = slice(height * j, height * (j + 1))
+        g_ref[at, column : column + LANES] = ref[0:height, LANES * j : LANES * (j + 1)]
+        right = ref[0:height, LANES * (j + 1) : LANES * (j + 2)] if j + 1 < pairs else nothing
+        left = ref[0:height, LANES * (j - 1) : LANES * j] if j > 0 else nothing
+        g_ref[at, column + LANES : column + 256] = jnp.where(low, right, left)
+
+
+def own_planes_kernel(own_ref, near_ref, xt_own_ref, xt_near_ref, d_ref, g_ref):
+    lay_out(own_ref, g_ref, 0)
+    lay_out(near_ref, g_ref, 256)
+    d = jnp.dot(xt_near_ref[...], g_ref[...], preferred_element_type=jnp.float32)
+    own = jnp.dot(xt_own_ref[...], g_ref[:, 0:256], preferred_element_type=jnp.float32)
+    d_ref[:, 0:256] = d[:, 0:256]
+    d_ref[:, 256:512] = d[:, 256:512] + own
+
+
+def kernel_gradient_kernel(core_ref, far_ref, g_ref, xt_own_ref, d_ref, slots_ref, g_far_ref, dw_ref):
+    lay_out(far_ref, g_far_ref, 0)
+    parts = (
+        d_ref[:, 0:256] + jnp.dot(xt_own_ref[...], g_far_ref[...], preferred_element_type=jnp.float32),
+        d_ref[:, 256:512],
+    )
     lo = lax.broadcasted_iota(jnp.int32, (CH, LANES), 1) < CH
     core_0 = jnp.full((CH, LANES), core_ref[0], jnp.int32) == 0
 
     def block(part, oh, parity, half):
         r = LANES * oh + CH * parity
-        c = 256 * part + LANES * half
-        return d[r : r + CH, c : c + LANES]
+        return parts[part][r : r + CH, LANES * half : LANES * (half + 1)]
 
     def swap(v):
         return pltpu.roll(v, CH, 1)
@@ -94,7 +107,7 @@
     def high_one(part, oh):
         return swap(block(part, oh, 1, 0)) + block(part, oh, 0, 1)
 
-    total = jnp.sum(g_ref[:, 256:384].astype(jnp.float32) + g_ref[:, 512:640].astype(jnp.float32), axis=0, keepdims=True)
+    total = jnp.sum(g_ref[:, 0:128].astype(jnp.float32) + g_ref[:, 256:384].astype(jnp.float32), axis=0, keepdims=True)
     first = lax.broadcasted_iota(jnp.int32, (CH, LANES), 0) == 0
     bias = jnp.where(first, jnp.broadcast_to(total + swap(total), (CH, LANES)), 0.0)
     blocks = (
@@ -117,13 +130,13 @@
         slots_ref[SLOT * i : SLOT * (i + 1), :] = to_slot(dw_ref[CHUNK * i : CHUNK * (i + 1), :], exponent)
 
 
-def input_gradient_kernel(g_ref, wt_ref, dx_ref):
+def input_gradient_kernel(g_far_ref, g_ref, wt_ref, dx_ref):
     height, packed = dx_ref.shape
     pairs = packed // LANES
     rows = pairs * height
-    y = lax.dot_general(
-        g_ref[...], wt_ref[...], (((1,), (1,)), ((), ())), preferred_element_type=jnp.float32
-    )
+    turn = (((1,), (1,)), ((), ()))
+    y = lax.dot_general(g_ref[...], wt_ref[:, 256:768], turn, preferred_element_type=jnp.float32)
+    y = y + lax.dot_general(g_far_ref[...], wt_ref[:, 0:256], turn, preferred_element_type=jnp.float32)
     h = lax.broadcasted_iota(jnp.int32, (rows, LANES), 0) % height
     up = jnp.where(h == height - 1, 0.0, pltpu.roll(y[:, :LANES], rows - 1, 0))
     down = jnp.where(h == 0, 0.0, pltpu.roll(y[:, 2 * LANES :], 1, 0))
@@ -164,25 +177,53 @@
         out_ref[SLOT * i : SLOT * (i + 1), :] = slot
 
 
-def unpack_kernel(core_ref, mine_slots_ref, other_slots_ref, weight_ref, bias_ref, mine_ref, other_ref):
-    for slots_ref, rows_ref in ((mine_slots_ref, mine_ref), (other_slots_ref, other_ref)):
-        for i in range(slots_ref.shape[0] // SLOT):
-            rows_ref[CHUNK * i : CHUNK * (i + 1), :] = from_slot(slots_ref, i)
-    core_0 = jnp.full((CH, LANES), core_ref[0], jnp.int32) == 0
-    places = (
-        ((19, 18), (22, 21), (25, 24), (20, 23), (26, 11), (10, 9), (13, 12)),
-        ((1, 0), (4, 3), (7, 6), (2, 5), (8, 17), (16, 15), (14, None)),
-    )
-    for half, sides in enumerate(places):
-        for i, (lower, upper) in enumerate(sides):
-            a = mine_ref[CH * i : CH * (i + 1), :]
-            b = other_ref[CH * i : CH * (i + 1), :]
-            v = jnp.where(core_0, a, b) if half == 0 else jnp.where(core_0, b, a)
-            weight_ref[lower] = v[:, :CH]
-            if upper is None:
-                bias_ref[...] = v[0:1, CH:]
-            else:
-                weight_ref[upper] = v[:, CH:]
+PLACES = (
+    (((19, 18), (22, 21), (25, 24), (20, 23), (26, 11), (10, 9), (13, 12)), ((18, 27), (9, 14))),
+    (((1, 0), (4, 3), (7, 6), (2, 5), (8, 17), (16, 15), (14, None)), ((0, 9), (14, 18))),
+)
+
+
+def unpack_half(half, slots_ref, weight_ref, bias_ref, rows_ref, taps_ref, last_ref, sems):
+    sides, ranges = PLACES[half]
+    for i in range(slots_ref.shape[0] // SLOT):
+        rows_ref[CHUNK * i : CHUNK * (i + 1), :] = from_slot(slots_ref, i)
+    stores = []
+    for i, (lower, upper) in enumerate(sides):
+        v = rows_ref[CH * i : CH * (i + 1), :]
+        taps_ref[lower] = v[:, :CH]
+        if upper is None:
+            last_ref[...] = v[0:1, CH:]
+            stores.append(pltpu.make_async_copy(last_ref, bias_ref, sems.at[2]))
+        else:
+            taps_ref[upper] = v[:, CH:]
+    for i, (first, end) in enumerate(ranges):
+        part = pl.ds(first, end - first)
+        stores.append(pltpu.make_async_copy(taps_ref.at[part], weight_ref.at[part], sems.at[i]))
+    for store in stores:
+        store.start()
+    for store in stores:
+        store.wait()
+
+
+def unpack_mine_kernel(core_ref, slots_ref, dx_ref, weight_ref, bias_ref, dx_out_ref, *scratch):
+    sems = scratch[-1]
+    dx_store = pltpu.make_async_copy(dx_ref, dx_out_ref, sems.at[3])
+    dx_store.start()
+    for half in range(2):
+
+        @pl.when(core_ref[0] == half)
+        def _():
+            unpack_half(half, slots_ref, weight_ref, bias_ref, *scratch)
+
+    dx_store.wait()
+
+
+def unpack_other_kernel(core_ref, slots_ref, _weight_ref, _bias_ref, weight_ref, bias_ref, *scratch):
+    for half in range(2):
+
+        @pl.when(core_ref[0] == 1 - half)
+        def _():
+            unpack_half(half, slots_ref, weight_ref, bias_ref, *scratch)
 
 
 def in_vmem(array):
@@ -243,17 +284,27 @@
             name="inputs",
         )(in_vmem(pair))
 
-    dw, g = pl.pallas_call(
+    xt_own = in_vmem(turned(pack))
+    d, g = pl.pallas_call(
+        own_planes_kernel,
+        out_shape=(
+            pltpu.VMEM((3 * LANES, 512), jnp.float32),
+            pltpu.VMEM((rows, 512), jnp.bfloat16),
+        ),
+        compiler_params=SMALL,
+        name="own_planes",
+    )(in_vmem(own), near, xt_own, in_vmem(turned(near)))
+    dw, g_far = pl.pallas_call(
         kernel_gradient_kernel,
-        in_specs=[in_smem] + [whole] * 5,
+        in_specs=[in_smem] + [whole] * 4,
         out_shape=(
             pltpu.VMEM((chips * SLOT, LANES), jnp.float32),
-            pltpu.VMEM((rows, 768), jnp.bfloat16),
+            pltpu.VMEM((rows, 256), jnp.bfloat16),
         ),
         scratch_shapes=[pltpu.VMEM((chips * CHUNK, LANES), jnp.float32)],
         compiler_params=SMALL,
         name="kernel_gradient",
-    )(core, in_vmem(far), in_vmem(own), near, in_vmem(turned(pack)), in_vmem(turned(near)))
+    )(core, in_vmem(far), in_vmem(g), xt_own, in_vmem(d))
     mine = pl.pallas_call(
         plane_sum_kernel,
         out_shape=pltpu.VMEM((groups * CHUNK, LANES), jnp.float32),
@@ -267,24 +318,43 @@
         name="finish",
     )(exchange(mine, "rep"))
     gathered = exchange_slots(total)
+    hbm = pl.BlockSpec(memory_space=pltpu.HBM)
+    grads = (
+        jax.ShapeDtypeStruct((27, CH, CH), jnp.float32),
+        jax.ShapeDtypeStruct((1, CH), jnp.float32),
+    )
+    scratch = [
+        pltpu.VMEM((chips * CHUNK, LANES), jnp.float32),
+        pltpu.VMEM((27, CH, CH), jnp.float32),
+        pltpu.VMEM((1, CH), jnp.float32),
+        pltpu.SemaphoreType.DMA((4,)),
+    ]
     other = lax.ppermute(gathered, "core", swap)
     dx = pl.pallas_call(
         input_gradient_kernel,
-        out_shape=jax.ShapeDtypeStruct((height, packed), jnp.bfloat16),
+        out_shape=pltpu.VMEM((height, packed), jnp.bfloat16),
         compiler_params=SMALL,
         name="input_gradient",
-    )(in_vmem(g), in_vmem(wt))
+    )(in_vmem(g_far), in_vmem(g), in_vmem(wt))
+    weight_grad, bias_grad, dx = pl.pallas_call(
+        unpack_mine_kernel,
+        in_specs=[in_smem, whole, whole],
+        out_specs=[hbm] * 3,
+        out_shape=grads + (jax.ShapeDtypeStruct((height, packed), jnp.bfloat16),),
+        scratch_shapes=scratch,
+        compiler_params=SMALL,
+        name="unpack_mine",
+    )(core, in_vmem(gathered.astype(jnp.float32)), in_vmem(dx))
     weight_grad, bias_grad = pl.pallas_call(
-        unpack_kernel,
-        in_specs=[in_smem, whole, whole],
-        out_shape=(
-            jax.ShapeDtypeStruct((27, CH, CH), jnp.float32),
-            jax.ShapeDtypeStruct((1, CH), jnp.float32),
-        ),
-        scratch_shapes=[pltpu.VMEM((chips * CHUNK, LANES), jnp.float32)] * 2,
-        compiler_params=SMALL,
-        name="unpack",
-    )(core, in_vmem(gathered.astype(jnp.float32)), in_vmem(other.astype(jnp.float32)))
+        unpack_other_kernel,
+        in_specs=[in_smem, whole, hbm, hbm],
+        out_specs=[hbm] * 2,
+        out_shape=grads,
+        scratch_shapes=scratch,
+        input_output_aliases={2: 0, 3: 1},
+        compiler_params=SMALL,
+        name="unpack_other",
+    )(core, in_vmem(other.astype(jnp.float32)), weight_grad, bias_grad)
     return dx.reshape(inputs.shape), weight_grad.reshape(3, 3, 3, CH, CH), bias_grad.reshape(CH)
 
 

time: 79.2 us -> 78.7 us (level)
  waiting for transfers between devices: 12.5 us -> 11.7 us
    ppermute x1, waiting for transfers between devices: 0.93 us -> 0.01 us  [on_device(): other = lax.ppermute(gathered, 'core', swap)]
    pallas_call x3 -> x5, Pallas kernels: 3.17 us -> 3.42 us  [the longest x1 0.95 us: on_device(): pl.pallas_call(unpack_other_kernel, in_specs=[in_smem, whole, hbm, hbm],...]
  transfers between devices with their start and end apart: 4 -> 4, of which waited for: 3 -> 2; matrix products, arithmetic and copies ran while one was open for 0% -> 0% of each run, Pallas kernels for 2% -> 3%
where the time goes in v6:
time: 78.7 us; the launch traced here: 78.4 us
  blocking collectives  34.5 us (44%)
  starting transfers between devices  25.3 us (32%)
  waiting for transfers between devices  11.7 us (15%)
  Pallas kernels  5.2 us (7%)
  between operations  0.8 us (1%)
    all_to_all x1, blocking collectives, exchange(): lax.all_to_all(rows.reshape(-1, 1, LANES), axis, 0, 0, tiled=True)  21.4 us
    all_to_all x1, blocking collectives, exchange_slots(): return lax.all_to_all(slots.astype(jnp.float16), 'chip', 0, 0, tiled=True)  13.1 us
    ppermute x1, starting transfers between devices, on_device(): near = in_vmem(lax.ppermute(pack, 'core', swap))  12.4 us
    all_to_all x1, waiting for transfers between devices, exchange_slots(): return lax.all_to_all(slots.astype(jnp.float16), 'chip', 0, 0, tiled=True)  8.34 us
    ppermute x1, starting transfers between devices, on_device(): other = lax.ppermute(gathered, 'core', swap)  7.16 us
    all_to_all x1, starting transfers between devices, exchange_slots(): return lax.all_to_all(slots.astype(jnp.float16), 'chip', 0, 0, tiled=True)  3.86 us
    ppermute x1, waiting for transfers between devices, on_device(): lax.ppermute(own, ('chip', 'core'), [(i, i + 1) for i in ends] + [(i + 1,...  3.37 us
    ppermute x1, starting transfers between devices, on_device(): lax.ppermute(own, ('chip', 'core'), [(i, i + 1) for i in ends] + [(i + 1,...  1.92 us
  transfers between devices with their start and end apart: 4, of which 2 were waited for; matrix products, arithmetic and copies ran while one was open for 0% of the time, Pallas kernels for 3%

profile of v6, /device:TPU:1, one launch (start us, length us, event | category | flops | bytes accessed | tf_op | source)
XLA Modules:
  0.0 78.4 jit_solution(11834588075587399132)
XLA Ops:
  0.6 1.1 %mask.1 = (bf16[16,4096]{1,0:T(8,128)(2,1)S(1)}, bf16[32,4096]{1,0:T(8,128)(2,1)S(1)}) custom-call(bf16[16,4096]{1,0:T(8,128)(2,1)} %bitcast.25, bf16[16,4096]{1,0:T(8,128)(2,1)} %bitcast.26, bf16[16,4096]{1,0:T(8,128)(2,1)} %bitcast.27), custom_call_target="tpu_custom_call" | custom-call | tf_op jit(solution)/shard_map/mask/pallas_call | solution.py:256
  1.7 12.4 %collective-permute-start.1 = (bf16[32,4096]{1,0:T(8,128)(2,1)S(1)}, bf16[32,4096]{1,0:T(8,128)(2,1)S(1)}, u32[]{:S(2)}, u32[]{:S(2)}) collective-permute-start(bf16[32,4096]{1,0:T(8,128)(2,1)S(1)} %get-tuple-element.15.pair_ref), channel_id=1, source_target_pairs={{0,1},{1,0},{2,3},{3,2},{4,5},{5,4},{6,7},{7,6},{8,9},{9,8},{10,11... | collective-permute-start | bytes 786440 | tf_op jit(solution)/shard_map/ppermute | solution.py:270
  14.1 1.9 %collective-permute-start = (bf16[16,4096]{1,0:T(8,128)(2,1)S(1)}, bf16[16,4096]{1,0:T(8,128)(2,1)S(1)}, u32[]{:S(2)}, u32[]{:S(2)}) collective-permute-start(bf16[16,4096]{1,0:T(8,128)(2,1)S(1)} %get-tuple-element.14.own_ref), channel_id=1, source_target_pairs={{1,2},{3,4},{5,6},{7,8},{9,10},{11,12},{13,14},{15,16},{17,18},{19... | collective-permute-start | bytes 393224 | tf_op jit(solution)/shard_map/ppermute | solution.py:269
  16.0 0.2 inputs.2.xt_own_ref
  16.3 0.0 collective-permute-done.1.pair_ref.near_ref
  16.3 0.2 inputs.3.xt_near_ref
  16.5 0.5 own_planes.1
  17.0 3.4 %collective-permute-done.far_ref = bf16[16,4096]{1,0:T(8,128)(2,1)S(1)} collective-permute-done((bf16[16,4096]{1,0:T(8,128)(2,1)S(1)}, bf16[16,4096]{1,0:T(8,128)(2,1)S(1)}, u32[]{:S(2)}, u32[]{:S(2)}) %collective-permute-start) | collective-permute-done | bytes 131104 | tf_op jit(solution)/shard_map/ppermute | solution.py:269
  20.4 0.4 kernel_gradient.1
  20.8 13.1 %all_to_all.26 = f16[32,16,128]{2,1,0:T(8,128)(2,1)S(1)} all-to-all(f16[32,16,128]{2,1,0:T(8,128)(2,1)S(1)} %bitcast.24), channel_id=1, replica_groups=mesh['rep'=12,'chip'=32,'core'=2] {'chip'}, dimensions={0} | all-to-all | bytes 262144 | tf_op jit(solution)/shard_map/all_to_all | solution.py:242
  34.1 21.4 %all_to_all.27 = f32[168,1,128]{2,1,0:T(1,128)S(1)} all-to-all(f32[168,1,128]{2,1,0:T(1,128)S(1)} %bitcast.20), channel_id=1, replica_groups=mesh['rep'=12,'chip'=32,'core'=2] {'rep'}, dimensions={0} | all-to-all | bytes 172032 | tf_op jit(solution)/shard_map/all_to_all | solution.py:238
  55.5 0.0 copy-start
  55.5 0.1 finish.1
  55.5 0.7 convert_element_type.20
  56.2 3.9 %all-to-all-start.2 = ((f16[32,16,128]{2,1,0:T(8,128)(2,1)}), f16[32,16,128]{2,1,0:T(8,128)(2,1)S(1)}, u32[]{:S(2)}, u32[]{:S(2)}) async-start(f16[32,16,128]{2,1,0:T(8,128)(2,1)} %bitcast.9), calls=%async_computation.2 | async-start | bytes 262144 | tf_op jit(solution)/shard_map/all_to_all | solution.py:242
  60.1 0.0 copy-done
  60.1 0.2 weights.1.wt_ref
  60.3 0.6 input_gradient.1.dx_ref
  60.9 8.3 %all-to-all-done.2 = f16[32,16,128]{2,1,0:T(8,128)(2,1)S(1)} async-done(((f16[32,16,128]{2,1,0:T(8,128)(2,1)}), f16[32,16,128]{2,1,0:T(8,128)(2,1)S(1)}, u32[]{:S(2)}, u32[]{:S(2)}) %all-to-all-start.2) | async-done | bytes 131104 | tf_op jit(solution)/shard_map/all_to_all | solution.py:242
  69.2 7.2 %collective-permute-start.2 = (f16[512,128]{1,0:T(8,128)(2,1)S(1)}, f16[512,128]{1,0:T(8,128)(2,1)S(1)}, u32[]{:S(2)}, u32[]{:S(2)}) collective-permute-start(f16[512,128]{1,0:T(8,128)(2,1)S(1)} %bitcast.23), channel_id=1, source_target_pairs={{0,1},{1,0},{2,3},{3,2},{4,5},{5,4},{6,7},{7,6},{8,9},{9,8},{10,11... | collective-permute-start | bytes 393224 | tf_op jit(solution)/shard_map/ppermute | solution.py:332
  76.4 0.9 %unpack_mine.1 = (f32[27,64,64]{2,1,0:T(8,128)}, f32[1,64]{1,0:T(1,128)}, bf16[16,4096]{1,0:T(8,128)(2,1)}) custom-call(s32[1]{0:T(128)} %bitcast.core_ref, f32[512,128]{1,0:T(8,128)S(1)} %bitcast_convert_fusion.1.slots_ref, bf16[16,4096]{1,0:T(8,128)(2,1)S(1)} %input_gradient.1.dx_ref), custom_call_target="tpu_custom_call" | custom-call | tf_op jit(solution)/shard_map/unpack_mine/pallas_call | solution.py:339
  77.4 0.0 collective-permute-done.2
  77.4 1.0 %unpack_other.1 = (f32[27,64,64]{2,1,0:T(8,128)}, f32[1,64]{1,0:T(1,128)}) custom-call(s32[1]{0:T(128)} %bitcast.core_ref, f32[512,128]{1,0:T(8,128)S(1)} %convert_element_type.22.slots_ref, f32[27,64,64]{2,1,0:T(8,128)} %get-tuple-element.21._weight_ref, f32[1,64]{1,0:T(1,128)} %get-tuple-element.22._bias_ref), custom_call_target="tpu_custom_call", output_to_operand_aliasing={{0}: (2, {}), {1}: (3, {})} | custom-call | tf_op jit(solution)/shard_map/unpack_other/pallas_call | solution.py:348
  (5 shorter events, 0.1 us)
Async XLA Ops:
  1.7 14.6 %collective-permute-start.1 = (bf16[32,4096]{1,0:T(8,128)(2,1)S(1)}, bf16[32,4096]{1,0:T(8,128)(2,1)S(1)}, u32[]{:S(2)}, u32[]{:S(2)}) collective-permute-start(bf16[32,4096]{1,0:T(8,128)(2,1)S(1)} %get-tuple-element.15.pair_ref), channel_id=1, source_target_pairs={{0,1},{1,0},{2,3},{3,2},{4,5},{5,4},{6,7},{7,6},{8,9},{9,8},{10,11... | collective-permute-start | bytes 786440 | tf_op jit(solution)/shard_map/ppermute | solution.py:270
  14.1 6.3 %collective-permute-start = (bf16[16,4096]{1,0:T(8,128)(2,1)S(1)}, bf16[16,4096]{1,0:T(8,128)(2,1)S(1)}, u32[]{:S(2)}, u32[]{:S(2)}) collective-permute-start(bf16[16,4096]{1,0:T(8,128)(2,1)S(1)} %get-tuple-element.14.own_ref), channel_id=1, source_target_pairs={{1,2},{3,4},{5,6},{7,8},{9,10},{11,12},{13,14},{15,16},{17,18},{19... | collective-permute-start | bytes 393224 | tf_op jit(solution)/shard_map/ppermute | solution.py:269
  55.5 4.6 %copy-start = (bf16[3,3,3,64,64]{4,3,2,1,0:T(8,128)(2,1)S(1)}, bf16[3,3,3,64,64]{4,3,2,1,0:T(8,128)(2,1)}, u32[]{:S(2)}) copy-start(bf16[3,3,3,64,64]{4,3,2,1,0:T(8,128)(2,1)} %param.7) | copy-start | bytes 663556
  56.2 13.0 %all-to-all-start.2 = ((f16[32,16,128]{2,1,0:T(8,128)(2,1)}), f16[32,16,128]{2,1,0:T(8,128)(2,1)S(1)}, u32[]{:S(2)}, u32[]{:S(2)}) async-start(f16[32,16,128]{2,1,0:T(8,128)(2,1)} %bitcast.9), calls=%async_computation.2 | async-start | bytes 262144 | tf_op jit(solution)/shard_map/all_to_all | solution.py:242
  69.2 8.2 %collective-permute-start.2 = (f16[512,128]{1,0:T(8,128)(2,1)S(1)}, f16[512,128]{1,0:T(8,128)(2,1)S(1)}, u32[]{:S(2)}, u32[]{:S(2)}) collective-permute-start(f16[512,128]{1,0:T(8,128)(2,1)S(1)} %bitcast.23), channel_id=1, source_target_pairs={{0,1},{1,0},{2,3},{3,2},{4,5},{5,4},{6,7},{7,6},{8,9},{9,8},{10,11... | collective-permute-start | bytes 393224 | tf_op jit(solution)/shard_map/ppermute | solution.py:332

commit v7 on v4

--- a/solution.py
+++ b/solution.py
@@ -60,27 +60,40 @@
                 wt_ref[r : r + CH, 256 * slot + LANES : 256 * (slot + 1)] = jnp.concatenate(parts[2:], axis=1)
 
 
-def kernel_gradient_kernel(core_ref, far_ref, own_ref, near_ref, xt_own_ref, xt_near_ref, slots_ref, g_ref, dw_ref):
-    height, packed = own_ref.shape
+def lay_out(ref, g_ref, column):
+    height, packed = g_ref.shape[0] * LANES // ref.shape[1], ref.shape[1]
     pairs = packed // LANES
     low = lax.broadcasted_iota(jnp.int32, (height, LANES), 1) < CH
-    for slot, ref in enumerate((far_ref, own_ref, near_ref)):
-        for j in range(pairs):
-            at = slice(height * j, height * (j + 1))
-            g_ref[at, 256 * slot : 256 * slot + LANES] = ref[0:height, LANES * j : LANES * (j + 1)]
-            nothing = jnp.zeros((height, LANES), jnp.bfloat16)
-            right = ref[0:height, LANES * (j + 1) : LANES * (j + 2)] if j + 1 < pairs else nothing
-            left = ref[0:height, LANES * (j - 1) : LANES * j] if j > 0 else nothing
-            g_ref[at, 256 * slot + LANES : 256 * (slot + 1)] = jnp.where(low, right, left)
-    d = jnp.dot(xt_own_ref[...], g_ref[:, 0:512], preferred_element_type=jnp.float32)
-    d = d + jnp.dot(xt_near_ref[...], g_ref[:, 256:768], preferred_element_type=jnp.float32)
+    nothing = jnp.zeros((height, LANES), jnp.bfloat16)
+    for j in range(pairs):
+        at = slice(height * j, height * (j + 1))
+        g_ref[at, column : column + LANES] = ref[0:height, LANES * j : LANES * (j + 1)]
+        right = ref[0:height, LANES * (j + 1) : LANES * (j + 2)] if j + 1 < pairs else nothing
+        left = ref[0:height, LANES * (j - 1) : LANES * j] if j > 0 else nothing
+        g_ref[at, column + LANES : column + 256] = jnp.where(low, right, left)
+
+
+def own_planes_kernel(own_ref, near_ref, xt_own_ref, xt_near_ref, d_ref, g_ref):
+    lay_out(own_ref, g_ref, 0)
+    lay_out(near_ref, g_ref, 256)
+    d = jnp.dot(xt_near_ref[...], g_ref[...], preferred_element_type=jnp.float32)
+    own = jnp.dot(xt_own_ref[...], g_ref[:, 0:256], preferred_element_type=jnp.float32)
+    d_ref[:, 0:256] = d[:, 0:256]
+    d_ref[:, 256:512] = d[:, 256:512] + own
+
+
+def kernel_gradient_kernel(core_ref, far_ref, g_ref, xt_own_ref, d_ref, slots_ref, g_far_ref, dw_ref):
+    lay_out(far_ref, g_far_ref, 0)
+    parts = (
+        d_ref[:, 0:256] + jnp.dot(xt_own_ref[...], g_far_ref[...], preferred_element_type=jnp.float32),
+        d_ref[:, 256:512],
+    )
     lo = lax.broadcasted_iota(jnp.int32, (CH, LANES), 1) < CH
     core_0 = jnp.full((CH, LANES), core_ref[0], jnp.int32) == 0
 
     def block(part, oh, parity, half):
         r = LANES * oh + CH * parity
-        c = 256 * part + LANES * half
-        return d[r : r + CH, c : c + LANES]
+        return parts[part][r : r + CH, LANES * half : LANES * (half + 1)]
 
     def swap(v):
         return pltpu.roll(v, CH, 1)
@@ -94,7 +107,7 @@
     def high_one(part, oh):
         return swap(block(part, oh, 1, 0)) + block(part, oh, 0, 1)
 
-    total = jnp.sum(g_ref[:, 256:384].astype(jnp.float32) + g_ref[:, 512:640].astype(jnp.float32), axis=0, keepdims=True)
+    total = jnp.sum(g_ref[:, 0:128].astype(jnp.float32) + g_ref[:, 256:384].astype(jnp.float32), axis=0, keepdims=True)
     first = lax.broadcasted_iota(jnp.int32, (CH, LANES), 0) == 0
     bias = jnp.where(first, jnp.broadcast_to(total + swap(total), (CH, LANES)), 0.0)
     blocks = (
@@ -117,13 +130,13 @@
         slots_ref[SLOT * i : SLOT * (i + 1), :] = to_slot(dw_ref[CHUNK * i : CHUNK * (i + 1), :], exponent)
 
 
-def input_gradient_kernel(g_ref, wt_ref, dx_ref):
+def input_gradient_kernel(g_far_ref, g_ref, wt_ref, dx_ref):
     height, packed = dx_ref.shape
     pairs = packed // LANES
     rows = pairs * height
-    y = lax.dot_general(
-        g_ref[...], wt_ref[...], (((1,), (1,)), ((), ())), preferred_element_type=jnp.float32
-    )
+    turn = (((1,), (1,)), ((), ()))
+    y = lax.dot_general(g_ref[...], wt_ref[:, 256:768], turn, preferred_element_type=jnp.float32)
+    y = y + lax.dot_general(g_far_ref[...], wt_ref[:, 0:256], turn, preferred_element_type=jnp.float32)
     h = lax.broadcasted_iota(jnp.int32, (rows, LANES), 0) % height
     up = jnp.where(h == height - 1, 0.0, pltpu.roll(y[:, :LANES], rows - 1, 0))
     down = jnp.where(h == 0, 0.0, pltpu.roll(y[:, 2 * LANES :], 1, 0))
@@ -256,17 +269,27 @@
             name="inputs",
         )(in_vmem(pair))
 
-    dw, g = pl.pallas_call(
+    xt_own = in_vmem(turned(pack))
+    d, g = pl.pallas_call(
+        own_planes_kernel,
+        out_shape=(
+            pltpu.VMEM((3 * LANES, 512), jnp.float32),
+            pltpu.VMEM((rows, 512), jnp.bfloat16),
+        ),
+        compiler_params=SMALL,
+        name="own_planes",
+    )(in_vmem(own), near, xt_own, in_vmem(turned(near)))
+    dw, g_far = pl.pallas_call(
         kernel_gradient_kernel,
-        in_specs=[in_smem] + [whole] * 5,
+        in_specs=[in_smem] + [whole] * 4,
         out_shape=(
             pltpu.VMEM((chips * SLOT, LANES), jnp.float32),
-            pltpu.VMEM((rows, 768), jnp.bfloat16),
+            pltpu.VMEM((rows, 256), jnp.bfloat16),
         ),
         scratch_shapes=[pltpu.VMEM((chips * CHUNK, LANES), jnp.float32)],
         compiler_params=SMALL,
         name="kernel_gradient",
-    )(core, in_vmem(far), in_vmem(own), near, in_vmem(turned(pack)), in_vmem(turned(near)))
+    )(core, in_vmem(far), in_vmem(g), xt_own, in_vmem(d))
     mine = pl.pallas_call(
         plane_sum_kernel,
         out_shape=pltpu.VMEM((groups * CHUNK, LANES), jnp.float32),
@@ -286,7 +309,7 @@
         out_shape=pltpu.VMEM((height, packed), jnp.bfloat16),
         compiler_params=SMALL,
         name="input_gradient",
-    )(in_vmem(g), in_vmem(wt))
+    )(in_vmem(g_far), in_vmem(g), in_vmem(wt))
     weight_grad, bias_grad, dx = pl.pallas_call(
         unpack_kernel,
         in_specs=[in_smem, whole, whole, whole],

time: 79.2 us -> 78.8 us (level)
  no operation moved by 1% of the time
where the time goes in v7:
time: 78.8 us; the launch traced here: 78.5 us
  blocking collectives  34.5 us (44%)
  starting transfers between devices  25.3 us (32%)
  waiting for transfers between devices  12.6 us (16%)
  Pallas kernels  4.43 us (6%)
    all_to_all x1, blocking collectives, exchange(): lax.all_to_all(rows.reshape(-1, 1, LANES), axis, 0, 0, tiled=True)  21.4 us
    all_to_all x1, blocking collectives, exchange_slots(): return lax.all_to_all(slots.astype(jnp.float16), 'chip', 0, 0, tiled=True)  13.1 us
    ppermute x1, starting transfers between devices, on_device(): near = in_vmem(lax.ppermute(pack, 'core', swap))  12.4 us
    all_to_all x1, waiting for transfers between devices, exchange_slots(): return lax.all_to_all(slots.astype(jnp.float16), 'chip', 0, 0, tiled=True)  8.34 us
    ppermute x1, starting transfers between devices, on_device(): other = lax.ppermute(gathered, 'core', swap)  7.16 us
    all_to_all x1, starting transfers between devices, exchange_slots(): return lax.all_to_all(slots.astype(jnp.float16), 'chip', 0, 0, tiled=True)  3.86 us
    ppermute x1, waiting for transfers between devices, on_device(): lax.ppermute(own, ('chip', 'core'), [(i, i + 1) for i in ends] + [(i + 1,...  3.37 us
    ppermute x1, starting transfers between devices, on_device(): lax.ppermute(own, ('chip', 'core'), [(i, i + 1) for i in ends] + [(i + 1,...  1.92 us
  transfers between devices with their start and end apart: 4, of which 3 were waited for; matrix products, arithmetic and copies ran while one was open for 0% of the time, Pallas kernels for 2%

profile of v7, /device:TPU:1, one launch (start us, length us, event | category | flops | bytes accessed | tf_op | source)
XLA Modules:
  0.0 78.5 jit_solution(7590026459494294104)
XLA Ops:
  0.6 1.1 %mask.1 = (bf16[16,4096]{1,0:T(8,128)(2,1)S(1)}, bf16[32,4096]{1,0:T(8,128)(2,1)S(1)}) custom-call(bf16[16,4096]{1,0:T(8,128)(2,1)} %bitcast.24, bf16[16,4096]{1,0:T(8,128)(2,1)} %bitcast.25, bf16[16,4096]{1,0:T(8,128)(2,1)} %bitcast.26), custom_call_target="tpu_custom_call" | custom-call | tf_op jit(solution)/shard_map/mask/pallas_call | solution.py:241
  1.7 12.4 %collective-permute-start.1 = (bf16[32,4096]{1,0:T(8,128)(2,1)S(1)}, bf16[32,4096]{1,0:T(8,128)(2,1)S(1)}, u32[]{:S(2)}, u32[]{:S(2)}) collective-permute-start(bf16[32,4096]{1,0:T(8,128)(2,1)S(1)} %get-tuple-element.13.pair_ref), channel_id=1, source_target_pairs={{0,1},{1,0},{2,3},{3,2},{4,5},{5,4},{6,7},{7,6},{8,9},{9,8},{10,11... | collective-permute-start | bytes 786440 | tf_op jit(solution)/shard_map/ppermute | solution.py:255
  14.1 1.9 %collective-permute-start = (bf16[16,4096]{1,0:T(8,128)(2,1)S(1)}, bf16[16,4096]{1,0:T(8,128)(2,1)S(1)}, u32[]{:S(2)}, u32[]{:S(2)}) collective-permute-start(bf16[16,4096]{1,0:T(8,128)(2,1)S(1)} %get-tuple-element.12.own_ref), channel_id=1, source_target_pairs={{1,2},{3,4},{5,6},{7,8},{9,10},{11,12},{13,14},{15,16},{17,18},{19... | collective-permute-start | bytes 393224 | tf_op jit(solution)/shard_map/ppermute | solution.py:254
  16.0 0.2 inputs.2.xt_own_ref
  16.3 0.0 collective-permute-done.1.pair_ref.near_ref
  16.3 0.2 inputs.3.xt_near_ref
  16.5 0.5 own_planes.1
  17.0 3.4 %collective-permute-done.far_ref = bf16[16,4096]{1,0:T(8,128)(2,1)S(1)} collective-permute-done((bf16[16,4096]{1,0:T(8,128)(2,1)S(1)}, bf16[16,4096]{1,0:T(8,128)(2,1)S(1)}, u32[]{:S(2)}, u32[]{:S(2)}) %collective-permute-start) | collective-permute-done | bytes 131104 | tf_op jit(solution)/shard_map/ppermute | solution.py:254
  20.4 0.4 kernel_gradient.1
  20.8 13.1 %all_to_all.26 = f16[32,16,128]{2,1,0:T(8,128)(2,1)S(1)} all-to-all(f16[32,16,128]{2,1,0:T(8,128)(2,1)S(1)} %bitcast.23), channel_id=1, replica_groups=mesh['rep'=12,'chip'=32,'core'=2] {'chip'}, dimensions={0} | all-to-all | bytes 262144 | tf_op jit(solution)/shard_map/all_to_all | solution.py:227
  34.1 21.4 %all_to_all.27 = f32[168,1,128]{2,1,0:T(1,128)S(1)} all-to-all(f32[168,1,128]{2,1,0:T(1,128)S(1)} %bitcast.20), channel_id=1, replica_groups=mesh['rep'=12,'chip'=32,'core'=2] {'rep'}, dimensions={0} | all-to-all | bytes 172032 | tf_op jit(solution)/shard_map/all_to_all | solution.py:223
  55.5 0.0 copy-start
  55.5 0.1 finish.1
  55.5 0.7 convert_element_type.20
  56.2 3.9 %all-to-all-start.2 = ((f16[32,16,128]{2,1,0:T(8,128)(2,1)}), f16[32,16,128]{2,1,0:T(8,128)(2,1)S(1)}, u32[]{:S(2)}, u32[]{:S(2)}) async-start(f16[32,16,128]{2,1,0:T(8,128)(2,1)} %bitcast.9), calls=%async_computation.2 | async-start | bytes 262144 | tf_op jit(solution)/shard_map/all_to_all | solution.py:227
  60.1 0.0 copy-done
  60.1 0.2 weights.1.wt_ref
  60.3 0.6 input_gradient.1.dx_ref
  60.9 8.3 %all-to-all-done.2 = f16[32,16,128]{2,1,0:T(8,128)(2,1)S(1)} async-done(((f16[32,16,128]{2,1,0:T(8,128)(2,1)}), f16[32,16,128]{2,1,0:T(8,128)(2,1)S(1)}, u32[]{:S(2)}, u32[]{:S(2)}) %all-to-all-start.2) | async-done | bytes 131104 | tf_op jit(solution)/shard_map/all_to_all | solution.py:227
  69.2 7.2 %collective-permute-start.2 = (f16[512,128]{1,0:T(8,128)(2,1)S(1)}, f16[512,128]{1,0:T(8,128)(2,1)S(1)}, u32[]{:S(2)}, u32[]{:S(2)}) collective-permute-start(f16[512,128]{1,0:T(8,128)(2,1)S(1)} %bitcast.22), channel_id=1, source_target_pairs={{0,1},{1,0},{2,3},{3,2},{4,5},{5,4},{6,7},{7,6},{8,9},{9,8},{10,11... | collective-permute-start | bytes 393224 | tf_op jit(solution)/shard_map/ppermute | solution.py:306
  76.4 0.9 %collective-permute-done.2 = f16[512,128]{1,0:T(8,128)(2,1)S(1)} collective-permute-done((f16[512,128]{1,0:T(8,128)(2,1)S(1)}, f16[512,128]{1,0:T(8,128)(2,1)S(1)}, u32[]{:S(2)}, u32[]{:S(2)}) %collective-permute-start.2) | collective-permute-done | bytes 131104 | tf_op jit(solution)/shard_map/ppermute | solution.py:306
  77.4 1.1 %unpack.1 = (f32[27,64,64]{2,1,0:T(8,128)}, f32[1,64]{1,0:T(1,128)}, bf16[16,4096]{1,0:T(8,128)(2,1)}) custom-call(s32[1]{0:T(128)} %bitcast.core_ref, f32[512,128]{1,0:T(8,128)S(1)} %bitcast_convert_fusion.1.mine_ref, f32[512,128]{1,0:T(8,128)S(1)} %convert_element_type.22.other_ref, bf16[16,4096]{1,0:T(8,128)(2,1)S(1)} %input_gradient.1.dx_ref), custom_call_target="tpu_custom_call" | custom-call | tf_op jit(solution)/shard_map/unpack/pallas_call | solution.py:313
  (5 shorter events, 0.1 us)
Async XLA Ops:
  1.7 14.6 %collective-permute-start.1 = (bf16[32,4096]{1,0:T(8,128)(2,1)S(1)}, bf16[32,4096]{1,0:T(8,128)(2,1)S(1)}, u32[]{:S(2)}, u32[]{:S(2)}) collective-permute-start(bf16[32,4096]{1,0:T(8,128)(2,1)S(1)} %get-tuple-element.13.pair_ref), channel_id=1, source_target_pairs={{0,1},{1,0},{2,3},{3,2},{4,5},{5,4},{6,7},{7,6},{8,9},{9,8},{10,11... | collective-permute-start | bytes 786440 | tf_op jit(solution)/shard_map/ppermute | solution.py:255
  14.1 6.3 %collective-permute-start = (bf16[16,4096]{1,0:T(8,128)(2,1)S(1)}, bf16[16,4096]{1,0:T(8,128)(2,1)S(1)}, u32[]{:S(2)}, u32[]{:S(2)}) collective-permute-start(bf16[16,4096]{1,0:T(8,128)(2,1)S(1)} %get-tuple-element.12.own_ref), channel_id=1, source_target_pairs={{1,2},{3,4},{5,6},{7,8},{9,10},{11,12},{13,14},{15,16},{17,18},{19... | collective-permute-start | bytes 393224 | tf_op jit(solution)/shard_map/ppermute | solution.py:254
  55.5 4.6 %copy-start = (bf16[3,3,3,64,64]{4,3,2,1,0:T(8,128)(2,1)S(1)}, bf16[3,3,3,64,64]{4,3,2,1,0:T(8,128)(2,1)}, u32[]{:S(2)}) copy-start(bf16[3,3,3,64,64]{4,3,2,1,0:T(8,128)(2,1)} %param.7) | copy-start | bytes 663556
  56.2 13.0 %all-to-all-start.2 = ((f16[32,16,128]{2,1,0:T(8,128)(2,1)}), f16[32,16,128]{2,1,0:T(8,128)(2,1)S(1)}, u32[]{:S(2)}, u32[]{:S(2)}) async-start(f16[32,16,128]{2,1,0:T(8,128)(2,1)} %bitcast.9), calls=%async_computation.2 | async-start | bytes 262144 | tf_op jit(solution)/shard_map/all_to_all | solution.py:227
  69.2 8.1 %collective-permute-start.2 = (f16[512,128]{1,0:T(8,128)(2,1)S(1)}, f16[512,128]{1,0:T(8,128)(2,1)S(1)}, u32[]{:S(2)}, u32[]{:S(2)}) collective-permute-start(f16[512,128]{1,0:T(8,128)(2,1)S(1)} %bitcast.22), channel_id=1, source_target_pairs={{0,1},{1,0},{2,3},{3,2},{4,5},{5,4},{6,7},{7,6},{8,9},{9,8},{10,11... | collective-permute-start | bytes 393224 | tf_op jit(solution)/shard_map/ppermute | solution.py:306

commit v8 on v7

--- a/solution.py
+++ b/solution.py
@@ -14,20 +14,30 @@
 
 
 def mask_kernel(preact_ref, grad_ref, x_ref, own_ref, pack_ref, z_ref, dy_ref, sems):
-    height = own_ref.shape[0]
-    loads = (
-        pltpu.make_async_copy(preact_ref, z_ref, sems.at[0]),
-        pltpu.make_async_copy(grad_ref, dy_ref, sems.at[1]),
-        pltpu.make_async_copy(x_ref, pack_ref.at[height:], sems.at[2]),
-    )
-    for load in loads:
-        load.start()
-    loads[0].wait()
-    loads[1].wait()
-    own = jnp.where(z_ref[...] > 0, dy_ref[...], jnp.zeros_like(dy_ref))
-    own_ref[...] = own
-    pack_ref[0:height, :] = own
-    loads[2].wait()
+    height, packed = own_ref.shape
+    pieces = sems.shape[1]
+    columns = [pl.ds(i * (packed // pieces), packed // pieces) for i in range(pieces)]
+    loads = [
+        (
+            pltpu.make_async_copy(preact_ref.at[:, part], z_ref.at[:, part], sems.at[0, i]),
+            pltpu.make_async_copy(grad_ref.at[:, part], dy_ref.at[:, part], sems.at[1, i]),
+            pltpu.make_async_copy(x_ref.at[:, part], pack_ref.at[height:, part], sems.at[2, i]),
+        )
+        for i, part in enumerate(columns)
+    ]
+    for z_load, dy_load, _ in loads:
+        z_load.start()
+        dy_load.start()
+    for _, _, x_load in loads:
+        x_load.start()
+    for part, (z_load, dy_load, _) in zip(columns, loads):
+        z_load.wait()
+        dy_load.wait()
+        own = jnp.where(z_ref[:, part] > 0, dy_ref[:, part], jnp.zeros((height, packed // pieces), own_ref.dtype))
+        own_ref[:, part] = own
+        pack_ref[0:height, part] = own
+    for _, _, x_load in loads:
+        x_load.wait()
 
 
 def inputs_kernel(pair_ref, xt_ref):
@@ -245,7 +255,7 @@
             pltpu.VMEM((height, packed), jnp.bfloat16),
             pltpu.VMEM((2 * height, packed), jnp.bfloat16),
         ),
-        scratch_shapes=[pltpu.VMEM((height, packed), jnp.bfloat16)] * 2 + [pltpu.SemaphoreType.DMA((3,))],
+        scratch_shapes=[pltpu.VMEM((height, packed), jnp.bfloat16)] * 2 + [pltpu.SemaphoreType.DMA((3, 4))],
         compiler_params=SMALL,
         name="mask",
     )(*(in_hbm(a.reshape(height, packed)) for a in (preact, grad_out, inputs)))

time: 78.8 us -> 78.9 us (level)
  no operation moved by 1% of the time
where the time goes in v8:
time: 78.9 us; the launch traced here: 78.5 us
  blocking collectives  34.5 us (44%)
  starting transfers between devices  25.3 us (32%)
  waiting for transfers between devices  12.6 us (16%)
  Pallas kernels  4.42 us (6%)
    all_to_all x1, blocking collectives, exchange(): lax.all_to_all(rows.reshape(-1, 1, LANES), axis, 0, 0, tiled=True)  21.4 us
    all_to_all x1, blocking collectives, exchange_slots(): return lax.all_to_all(slots.astype(jnp.float16), 'chip', 0, 0, tiled=True)  13.1 us
    ppermute x1, starting transfers between devices, on_device(): near = in_vmem(lax.ppermute(pack, 'core', swap))  12.4 us
    all_to_all x1, waiting for transfers between devices, exchange_slots(): return lax.all_to_all(slots.astype(jnp.float16), 'chip', 0, 0, tiled=True)  8.34 us
    ppermute x1, starting transfers between devices, on_device(): other = lax.ppermute(gathered, 'core', swap)  7.17 us
    all_to_all x1, starting transfers between devices, exchange_slots(): return lax.all_to_all(slots.astype(jnp.float16), 'chip', 0, 0, tiled=True)  3.86 us
    ppermute x1, waiting for transfers between devices, on_device(): lax.ppermute(own, ('chip', 'core'), [(i, i + 1) for i in ends] + [(i + 1,...  3.37 us
    ppermute x1, starting transfers between devices, on_device(): lax.ppermute(own, ('chip', 'core'), [(i, i + 1) for i in ends] + [(i + 1,...  1.92 us
  transfers between devices with their start and end apart: 4, of which 3 were waited for; matrix products, arithmetic and copies ran while one was open for 0% of the time, Pallas kernels for 2%

profile of v8, /device:TPU:1, one launch (start us, length us, event | category | flops | bytes accessed | tf_op | source)
XLA Modules:
  0.0 78.5 jit_solution(3315785167745115243)
XLA Ops:
  0.6 1.0 %mask.1 = (bf16[16,4096]{1,0:T(8,128)(2,1)S(1)}, bf16[32,4096]{1,0:T(8,128)(2,1)S(1)}) custom-call(bf16[16,4096]{1,0:T(8,128)(2,1)} %bitcast.24, bf16[16,4096]{1,0:T(8,128)(2,1)} %bitcast.25, bf16[16,4096]{1,0:T(8,128)(2,1)} %bitcast.26), custom_call_target="tpu_custom_call" | custom-call | tf_op jit(solution)/shard_map/mask/pallas_call | solution.py:251
  1.7 12.4 %collective-permute-start.1 = (bf16[32,4096]{1,0:T(8,128)(2,1)S(1)}, bf16[32,4096]{1,0:T(8,128)(2,1)S(1)}, u32[]{:S(2)}, u32[]{:S(2)}) collective-permute-start(bf16[32,4096]{1,0:T(8,128)(2,1)S(1)} %get-tuple-element.13.pair_ref), channel_id=1, source_target_pairs={{0,1},{1,0},{2,3},{3,2},{4,5},{5,4},{6,7},{7,6},{8,9},{9,8},{10,11... | collective-permute-start | bytes 786440 | tf_op jit(solution)/shard_map/ppermute | solution.py:265
  14.1 1.9 %collective-permute-start = (bf16[16,4096]{1,0:T(8,128)(2,1)S(1)}, bf16[16,4096]{1,0:T(8,128)(2,1)S(1)}, u32[]{:S(2)}, u32[]{:S(2)}) collective-permute-start(bf16[16,4096]{1,0:T(8,128)(2,1)S(1)} %get-tuple-element.12.own_ref), channel_id=1, source_target_pairs={{1,2},{3,4},{5,6},{7,8},{9,10},{11,12},{13,14},{15,16},{17,18},{19... | collective-permute-start | bytes 393224 | tf_op jit(solution)/shard_map/ppermute | solution.py:264
  16.0 0.2 inputs.2.xt_own_ref
  16.2 0.0 collective-permute-done.1.pair_ref.near_ref
  16.2 0.2 inputs.3.xt_near_ref
  16.5 0.5 own_planes.1
  17.0 3.4 %collective-permute-done.far_ref = bf16[16,4096]{1,0:T(8,128)(2,1)S(1)} collective-permute-done((bf16[16,4096]{1,0:T(8,128)(2,1)S(1)}, bf16[16,4096]{1,0:T(8,128)(2,1)S(1)}, u32[]{:S(2)}, u32[]{:S(2)}) %collective-permute-start) | collective-permute-done | bytes 131104 | tf_op jit(solution)/shard_map/ppermute | solution.py:264
  20.4 0.4 kernel_gradient.1
  20.8 13.1 %all_to_all.26 = f16[32,16,128]{2,1,0:T(8,128)(2,1)S(1)} all-to-all(f16[32,16,128]{2,1,0:T(8,128)(2,1)S(1)} %bitcast.23), channel_id=1, replica_groups=mesh['rep'=12,'chip'=32,'core'=2] {'chip'}, dimensions={0} | all-to-all | bytes 262144 | tf_op jit(solution)/shard_map/all_to_all | solution.py:237
  34.0 21.4 %all_to_all.27 = f32[168,1,128]{2,1,0:T(1,128)S(1)} all-to-all(f32[168,1,128]{2,1,0:T(1,128)S(1)} %bitcast.20), channel_id=1, replica_groups=mesh['rep'=12,'chip'=32,'core'=2] {'rep'}, dimensions={0} | all-to-all | bytes 172032 | tf_op jit(solution)/shard_map/all_to_all | solution.py:233
  55.5 0.0 copy-start
  55.5 0.1 finish.1
  55.5 0.7 convert_element_type.20
  56.2 3.9 %all-to-all-start.2 = ((f16[32,16,128]{2,1,0:T(8,128)(2,1)}), f16[32,16,128]{2,1,0:T(8,128)(2,1)S(1)}, u32[]{:S(2)}, u32[]{:S(2)}) async-start(f16[32,16,128]{2,1,0:T(8,128)(2,1)} %bitcast.9), calls=%async_computation.2 | async-start | bytes 262144 | tf_op jit(solution)/shard_map/all_to_all | solution.py:237
  60.1 0.0 copy-done
  60.1 0.2 weights.1.wt_ref
  60.3 0.6 input_gradient.1.dx_ref
  60.9 8.3 %all-to-all-done.2 = f16[32,16,128]{2,1,0:T(8,128)(2,1)S(1)} async-done(((f16[32,16,128]{2,1,0:T(8,128)(2,1)}), f16[32,16,128]{2,1,0:T(8,128)(2,1)S(1)}, u32[]{:S(2)}, u32[]{:S(2)}) %all-to-all-start.2) | async-done | bytes 131104 | tf_op jit(solution)/shard_map/all_to_all | solution.py:237
  69.2 7.2 %collective-permute-start.2 = (f16[512,128]{1,0:T(8,128)(2,1)S(1)}, f16[512,128]{1,0:T(8,128)(2,1)S(1)}, u32[]{:S(2)}, u32[]{:S(2)}) collective-permute-start(f16[512,128]{1,0:T(8,128)(2,1)S(1)} %bitcast.22), channel_id=1, source_target_pairs={{0,1},{1,0},{2,3},{3,2},{4,5},{5,4},{6,7},{7,6},{8,9},{9,8},{10,11... | collective-permute-start | bytes 393224 | tf_op jit(solution)/shard_map/ppermute | solution.py:316
  76.4 0.9 %collective-permute-done.2 = f16[512,128]{1,0:T(8,128)(2,1)S(1)} collective-permute-done((f16[512,128]{1,0:T(8,128)(2,1)S(1)}, f16[512,128]{1,0:T(8,128)(2,1)S(1)}, u32[]{:S(2)}, u32[]{:S(2)}) %collective-permute-start.2) | collective-permute-done | bytes 131104 | tf_op jit(solution)/shard_map/ppermute | solution.py:316
  77.4 1.1 %unpack.1 = (f32[27,64,64]{2,1,0:T(8,128)}, f32[1,64]{1,0:T(1,128)}, bf16[16,4096]{1,0:T(8,128)(2,1)}) custom-call(s32[1]{0:T(128)} %bitcast.core_ref, f32[512,128]{1,0:T(8,128)S(1)} %bitcast_convert_fusion.1.mine_ref, f32[512,128]{1,0:T(8,128)S(1)} %convert_element_type.22.other_ref, bf16[16,4096]{1,0:T(8,128)(2,1)S(1)} %input_gradient.1.dx_ref), custom_call_target="tpu_custom_call" | custom-call | tf_op jit(solution)/shard_map/unpack/pallas_call | solution.py:323
  (5 shorter events, 0.1 us)
Async XLA Ops:
  1.7 14.6 %collective-permute-start.1 = (bf16[32,4096]{1,0:T(8,128)(2,1)S(1)}, bf16[32,4096]{1,0:T(8,128)(2,1)S(1)}, u32[]{:S(2)}, u32[]{:S(2)}) collective-permute-start(bf16[32,4096]{1,0:T(8,128)(2,1)S(1)} %get-tuple-element.13.pair_ref), channel_id=1, source_target_pairs={{0,1},{1,0},{2,3},{3,2},{4,5},{5,4},{6,7},{7,6},{8,9},{9,8},{10,11... | collective-permute-start | bytes 786440 | tf_op jit(solution)/shard_map/ppermute | solution.py:265
  14.1 6.3 %collective-permute-start = (bf16[16,4096]{1,0:T(8,128)(2,1)S(1)}, bf16[16,4096]{1,0:T(8,128)(2,1)S(1)}, u32[]{:S(2)}, u32[]{:S(2)}) collective-permute-start(bf16[16,4096]{1,0:T(8,128)(2,1)S(1)} %get-tuple-element.12.own_ref), channel_id=1, source_target_pairs={{1,2},{3,4},{5,6},{7,8},{9,10},{11,12},{13,14},{15,16},{17,18},{19... | collective-permute-start | bytes 393224 | tf_op jit(solution)/shard_map/ppermute | solution.py:264
  55.5 4.6 %copy-start = (bf16[3,3,3,64,64]{4,3,2,1,0:T(8,128)(2,1)S(1)}, bf16[3,3,3,64,64]{4,3,2,1,0:T(8,128)(2,1)}, u32[]{:S(2)}) copy-start(bf16[3,3,3,64,64]{4,3,2,1,0:T(8,128)(2,1)} %param.7) | copy-start | bytes 663556
  56.2 13.0 %all-to-all-start.2 = ((f16[32,16,128]{2,1,0:T(8,128)(2,1)}), f16[32,16,128]{2,1,0:T(8,128)(2,1)S(1)}, u32[]{:S(2)}, u32[]{:S(2)}) async-start(f16[32,16,128]{2,1,0:T(8,128)(2,1)} %bitcast.9), calls=%async_computation.2 | async-start | bytes 262144 | tf_op jit(solution)/shard_map/all_to_all | solution.py:237
  69.2 8.1 %collective-permute-start.2 = (f16[512,128]{1,0:T(8,128)(2,1)S(1)}, f16[512,128]{1,0:T(8,128)(2,1)S(1)}, u32[]{:S(2)}, u32[]{:S(2)}) collective-permute-start(f16[512,128]{1,0:T(8,128)(2,1)S(1)} %bitcast.22), channel_id=1, source_target_pairs={{0,1},{1,0},{2,3},{3,2},{4,5},{5,4},{6,7},{7,6},{8,9},{9,8},{10,11... | collective-permute-start | bytes 393224 | tf_op jit(solution)/shard_map/ppermute | solution.py:316

commit v9 on v7

--- a/solution.py
+++ b/solution.py
@@ -178,22 +178,18 @@
 
 
 def unpack_kernel(
-    core_ref, mine_ref, other_ref, dx_ref, weight_ref, bias_ref, dx_out_ref, rows_ref, taps_ref, last_ref, sems
+    slots_ref, dx_ref, weight_ref, bias_ref, dx_out_ref, rows_ref, taps_ref, last_ref, sems
 ):
     stores = [pltpu.make_async_copy(dx_ref, dx_out_ref, sems.at[0])]
     stores[0].start()
-    chips = mine_ref.shape[0] // SLOT
+    chips = slots_ref.shape[0] // (2 * SLOT)
     places = (
         (((19, 18), (22, 21), (25, 24), (20, 23), (26, 11), (10, 9), (13, 12)), ((18, 27), (9, 14))),
         (((1, 0), (4, 3), (7, 6), (2, 5), (8, 17), (16, 15), (14, None)), ((0, 9), (14, 18))),
     )
-    core_0 = jnp.full((SLOT, LANES), core_ref[0], jnp.int32) == 0
     for core, (sides, ranges) in enumerate(places):
         for i in range(chips):
-            a = mine_ref[SLOT * i : SLOT * (i + 1), :]
-            b = other_ref[SLOT * i : SLOT * (i + 1), :]
-            v = jnp.where(core_0, a, b) if core == 0 else jnp.where(core_0, b, a)
-            rows_ref[CHUNK * i : CHUNK * (i + 1), :] = v[:CHUNK] * jnp.exp2(v[CHUNK : CHUNK + 1])
+            rows_ref[CHUNK * i : CHUNK * (i + 1), :] = from_slot(slots_ref, 2 * i + core)
         for i, (lower, upper) in enumerate(sides):
             v = rows_ref[CH * i : CH * (i + 1), :]
             taps_ref[lower] = v[:, :CH]
@@ -223,8 +219,8 @@
     return in_vmem(lax.all_to_all(rows.reshape(-1, 1, LANES), axis, 0, 0, tiled=True).reshape(-1, LANES))
 
 
-def exchange_slots(slots):
-    return lax.all_to_all(slots.astype(jnp.float16), "chip", 0, 0, tiled=True)
+def exchange_slots(slots, axis):
+    return lax.all_to_all(slots.astype(jnp.float16), axis, 0, 0, tiled=True)
 
 
 def on_device(inputs, preact, grad_out, weight):
@@ -295,24 +291,24 @@
         out_shape=pltpu.VMEM((groups * CHUNK, LANES), jnp.float32),
         compiler_params=SMALL,
         name="plane_sum",
-    )(in_vmem(exchange_slots(dw).astype(jnp.float32)))
-    total = pl.pallas_call(
-        lambda p, o: finish_kernel(p, o, scale=scale),
-        out_shape=pltpu.VMEM((chips * SLOT, LANES), jnp.float32),
-        compiler_params=SMALL,
-        name="finish",
-    )(exchange(mine, "rep"))
-    gathered = exchange_slots(total)
-    other = lax.ppermute(gathered, "core", swap)
+    )(in_vmem(exchange_slots(dw, "chip").astype(jnp.float32)))
+    summed = exchange(mine, "rep")
     dx = pl.pallas_call(
         input_gradient_kernel,
         out_shape=pltpu.VMEM((height, packed), jnp.bfloat16),
         compiler_params=SMALL,
         name="input_gradient",
     )(in_vmem(g_far), in_vmem(g), in_vmem(wt))
+    total = pl.pallas_call(
+        lambda p, o: finish_kernel(p, o, scale=scale),
+        out_shape=pltpu.VMEM((slabs * SLOT, LANES), jnp.float32),
+        compiler_params=SMALL,
+        name="finish",
+    )(summed)
+    gathered = exchange_slots(total, ("chip", "core"))
     weight_grad, bias_grad, dx = pl.pallas_call(
         unpack_kernel,
-        in_specs=[in_smem, whole, whole, whole],
+        in_specs=[whole, whole],
         out_specs=[pl.BlockSpec(memory_space=pltpu.HBM)] * 3,
         out_shape=(
             jax.ShapeDtypeStruct((27, CH, CH), jnp.float32),
@@ -327,7 +323,7 @@
         ],
         compiler_params=SMALL,
         name="unpack",
-    )(core, in_vmem(gathered.astype(jnp.float32)), in_vmem(other.astype(jnp.float32)), in_vmem(dx))
+    )(in_vmem(gathered.astype(jnp.float32)), in_vmem(dx))
     return dx.reshape(inputs.shape), weight_grad.reshape(3, 3, 3, CH, CH), bias_grad.reshape(CH)
 
 

time: 78.8 us -> 78.1 us (level)
  starting transfers between devices: 25.3 us -> 22.6 us
  waiting for transfers between devices: 12.6 us -> 14.6 us
    ppermute x1 -> x0, starting transfers between devices: 7.16 us -> none  [on_device(): other = lax.ppermute(gathered, 'core', swap)]
    all_to_all x1, starting transfers between devices: 3.86 us -> 8.3 us  [exchange_slots(): return lax.all_to_all(slots.astype(jnp.float16), axis, 0, 0, tiled=True)]
    all_to_all x1, waiting for transfers between devices: 8.34 us -> 11.2 us  [exchange_slots(): return lax.all_to_all(slots.astype(jnp.float16), axis, 0, 0, tiled=True)]
    ppermute x1 -> x0, waiting for transfers between devices: 0.93 us -> none  [on_device(): other = lax.ppermute(gathered, 'core', swap)]
  transfers between devices with their start and end apart: 4 -> 3, of which waited for: 3 -> 2; matrix products, arithmetic and copies ran while one was open for 0% -> 0% of each run, Pallas kernels for 2% -> 2%
where the time goes in v9:
time: 78.1 us; the launch traced here: 77.8 us
  blocking collectives  34.5 us (44%)
  starting transfers between devices  22.6 us (29%)
  waiting for transfers between devices  14.6 us (19%)
  Pallas kernels  4.44 us (6%)
  other arithmetic  0.84 us (1%)
    all_to_all x1, blocking collectives, exchange(): lax.all_to_all(rows.reshape(-1, 1, LANES), axis, 0, 0, tiled=True)  21.4 us
    all_to_all x1, blocking collectives, exchange_slots(): return lax.all_to_all(slots.astype(jnp.float16), axis, 0, 0, tiled=True)  13.1 us
    ppermute x1, starting transfers between devices, on_device(): near = in_vmem(lax.ppermute(pack, 'core', swap))  12.4 us
    all_to_all x1, waiting for transfers between devices, exchange_slots(): return lax.all_to_all(slots.astype(jnp.float16), axis, 0, 0, tiled=True)  11.2 us
    all_to_all x1, starting transfers between devices, exchange_slots(): return lax.all_to_all(slots.astype(jnp.float16), axis, 0, 0, tiled=True)  8.3 us
    ppermute x1, waiting for transfers between devices, on_device(): lax.ppermute(own, ('chip', 'core'), [(i, i + 1) for i in ends] + [(i + 1,...  3.37 us
    ppermute x1, starting transfers between devices, on_device(): lax.ppermute(own, ('chip', 'core'), [(i, i + 1) for i in ends] + [(i + 1,...  1.92 us
  transfers between devices with their start and end apart: 3, of which 2 were waited for; matrix products, arithmetic and copies ran while one was open for 0% of the time, Pallas kernels for 2%

profile of v9, /device:TPU:1, one launch (start us, length us, event | category | flops | bytes accessed | tf_op | source)
XLA Modules:
  0.0 77.8 jit_solution(17868450238486003681)
XLA Ops:
  0.6 1.1 %mask.1 = (bf16[16,4096]{1,0:T(8,128)(2,1)S(1)}, bf16[32,4096]{1,0:T(8,128)(2,1)S(1)}) custom-call(bf16[16,4096]{1,0:T(8,128)(2,1)} %bitcast.24, bf16[16,4096]{1,0:T(8,128)(2,1)} %bitcast.25, bf16[16,4096]{1,0:T(8,128)(2,1)} %bitcast.26), custom_call_target="tpu_custom_call" | custom-call | tf_op jit(solution)/shard_map/mask/pallas_call | solution.py:237
  1.7 12.4 %collective-permute-start.1 = (bf16[32,4096]{1,0:T(8,128)(2,1)S(1)}, bf16[32,4096]{1,0:T(8,128)(2,1)S(1)}, u32[]{:S(2)}, u32[]{:S(2)}) collective-permute-start(bf16[32,4096]{1,0:T(8,128)(2,1)S(1)} %get-tuple-element.13.pair_ref), channel_id=1, source_target_pairs={{0,1},{1,0},{2,3},{3,2},{4,5},{5,4},{6,7},{7,6},{8,9},{9,8},{10,11... | collective-permute-start | bytes 786440 | tf_op jit(solution)/shard_map/ppermute | solution.py:251
  14.1 1.9 %collective-permute-start = (bf16[16,4096]{1,0:T(8,128)(2,1)S(1)}, bf16[16,4096]{1,0:T(8,128)(2,1)S(1)}, u32[]{:S(2)}, u32[]{:S(2)}) collective-permute-start(bf16[16,4096]{1,0:T(8,128)(2,1)S(1)} %get-tuple-element.12.own_ref), channel_id=1, source_target_pairs={{1,2},{3,4},{5,6},{7,8},{9,10},{11,12},{13,14},{15,16},{17,18},{19... | collective-permute-start | bytes 393224 | tf_op jit(solution)/shard_map/ppermute | solution.py:250
  16.0 0.2 inputs.2.xt_own_ref
  16.3 0.0 collective-permute-done.1.pair_ref.near_ref
  16.3 0.2 inputs.3.xt_near_ref
  16.5 0.5 own_planes.1
  17.0 3.4 %collective-permute-done.far_ref = bf16[16,4096]{1,0:T(8,128)(2,1)S(1)} collective-permute-done((bf16[16,4096]{1,0:T(8,128)(2,1)S(1)}, bf16[16,4096]{1,0:T(8,128)(2,1)S(1)}, u32[]{:S(2)}, u32[]{:S(2)}) %collective-permute-start) | collective-permute-done | bytes 131104 | tf_op jit(solution)/shard_map/ppermute | solution.py:250
  20.4 0.4 kernel_gradient.1
  20.8 13.1 %all_to_all.23 = f16[32,16,128]{2,1,0:T(8,128)(2,1)S(1)} all-to-all(f16[32,16,128]{2,1,0:T(8,128)(2,1)S(1)} %bitcast.23), channel_id=1, replica_groups=mesh['rep'=12,'chip'=32,'core'=2] {'chip'}, dimensions={0} | all-to-all | bytes 262144 | tf_op jit(solution)/shard_map/all_to_all | solution.py:223
  34.1 21.4 %all_to_all.24 = f32[168,1,128]{2,1,0:T(1,128)S(1)} all-to-all(f32[168,1,128]{2,1,0:T(1,128)S(1)} %bitcast.22), channel_id=1, replica_groups=mesh['rep'=12,'chip'=32,'core'=2] {'rep'}, dimensions={0} | all-to-all | bytes 172032 | tf_op jit(solution)/shard_map/all_to_all | solution.py:219
  55.5 0.1 finish.1
  55.5 0.7 convert_element_type.19
  56.3 0.0 copy-start
  56.3 8.3 %all-to-all-start.2 = ((f16[64,16,128]{2,1,0:T(8,128)(2,1)}), f16[64,16,128]{2,1,0:T(8,128)(2,1)S(1)}, u32[]{:S(2)}, u32[]{:S(2)}) async-start(f16[64,16,128]{2,1,0:T(8,128)(2,1)} %bitcast.9), calls=%async_computation.2 | async-start | bytes 524288 | tf_op jit(solution)/shard_map/all_to_all | solution.py:223
  64.6 0.0 copy-done
  64.6 0.2 weights.1.wt_ref
  64.8 0.6 input_gradient.1.dx_ref
  65.4 11.2 %all-to-all-done.2 = f16[64,16,128]{2,1,0:T(8,128)(2,1)S(1)} async-done(((f16[64,16,128]{2,1,0:T(8,128)(2,1)}), f16[64,16,128]{2,1,0:T(8,128)(2,1)S(1)}, u32[]{:S(2)}, u32[]{:S(2)}) %all-to-all-start.2) | async-done | bytes 262176 | tf_op jit(solution)/shard_map/all_to_all | solution.py:223
  76.6 0.1 bitcast_convert_fusion.slots_ref
  76.7 1.1 %unpack.1 = (f32[27,64,64]{2,1,0:T(8,128)}, f32[1,64]{1,0:T(1,128)}, bf16[16,4096]{1,0:T(8,128)(2,1)}) custom-call(f32[1024,128]{1,0:T(8,128)S(1)} %bitcast_convert_fusion.slots_ref, bf16[16,4096]{1,0:T(8,128)(2,1)S(1)} %input_gradient.1.dx_ref), custom_call_target="tpu_custom_call" | custom-call | tf_op jit(solution)/shard_map/unpack/pallas_call | solution.py:309
  (3 shorter events, 0.1 us)
Async XLA Ops:
  1.7 14.6 %collective-permute-start.1 = (bf16[32,4096]{1,0:T(8,128)(2,1)S(1)}, bf16[32,4096]{1,0:T(8,128)(2,1)S(1)}, u32[]{:S(2)}, u32[]{:S(2)}) collective-permute-start(bf16[32,4096]{1,0:T(8,128)(2,1)S(1)} %get-tuple-element.13.pair_ref), channel_id=1, source_target_pairs={{0,1},{1,0},{2,3},{3,2},{4,5},{5,4},{6,7},{7,6},{8,9},{9,8},{10,11... | collective-permute-start | bytes 786440 | tf_op jit(solution)/shard_map/ppermute | solution.py:251
  14.1 6.3 %collective-permute-start = (bf16[16,4096]{1,0:T(8,128)(2,1)S(1)}, bf16[16,4096]{1,0:T(8,128)(2,1)S(1)}, u32[]{:S(2)}, u32[]{:S(2)}) collective-permute-start(bf16[16,4096]{1,0:T(8,128)(2,1)S(1)} %get-tuple-element.12.own_ref), channel_id=1, source_target_pairs={{1,2},{3,4},{5,6},{7,8},{9,10},{11,12},{13,14},{15,16},{17,18},{19... | collective-permute-start | bytes 393224 | tf_op jit(solution)/shard_map/ppermute | solution.py:250
  56.3 8.3 %copy-start = (bf16[3,3,3,64,64]{4,3,2,1,0:T(8,128)(2,1)S(1)}, bf16[3,3,3,64,64]{4,3,2,1,0:T(8,128)(2,1)}, u32[]{:S(2)}) copy-start(bf16[3,3,3,64,64]{4,3,2,1,0:T(8,128)(2,1)} %param.7) | copy-start | bytes 663556
  56.3 20.3 %all-to-all-start.2 = ((f16[64,16,128]{2,1,0:T(8,128)(2,1)}), f16[64,16,128]{2,1,0:T(8,128)(2,1)S(1)}, u32[]{:S(2)}, u32[]{:S(2)}) async-start(f16[64,16,128]{2,1,0:T(8,128)(2,1)} %bitcast.9), calls=%async_computation.2 | async-start | bytes 524288 | tf_op jit(solution)/shard_map/all_to_all | solution.py:223
